TPU v7x, 32 devices: a whole 2x2x4 slice. The times are simulated.
32 devices in a mesh: cp: 4 (over y, x), grp: 8 (over z, core).
Axes of the slice: x: 2, y: 2, z: 4, core: 2. Of those that a mesh axis runs over, the one named last changes fastest.
Arguments:
- queries: bfloat16 [16, 512, 2048], P('grp', 'cp'), may hold values from -108 to 108
- keys: bfloat16 [16, 512, 2048], P('grp', 'cp'), may hold values from -4 to 4
- values: bfloat16 [16, 512, 2048], P('grp', 'cp'), may hold values from -6 to 6
- lengths: int32 [16], P('grp'), may hold values from 128 to 512
- frame_map: bfloat16 [2048, 2176], replicated, may hold values from -0.125 to 0.125
- proj_weight: bfloat16 [2176, 4096], P('grp', 'cp'), may hold values from -0.125 to 0.125
- head_weight: bfloat16 [4096, 256], P('cp'), may hold values from -0.375 to 0.375
- act_embed: float32 [7, 4096], P(None, 'cp'), may hold values from -0.5 to 0.5
- actions: int32 [16, 7], P('grp'), may hold values from 0 to 255
- action_mask: int32 [16, 7], P('grp'), may hold values 0 or 1
- group_ids: int32 [16], P('grp'), may hold values from 0 to 1
- rewards: float32 [16], P('grp'), may hold values from -6 to 6
Outputs:
- logprobs: float32 [16, 7], P('grp')
- grad_proj: bfloat16 [2176, 4096], P('grp', 'cp')
- grad_head: bfloat16 [4096, 256], P('cp')
All inputs are finite; a program needn't handle non-finite values. No bound on the sum of `action_mask` on one device may be relied on, other than what follows from the above.
Results may differ from a plain program's by a relative error of at most 0.018.
Values may be sent and summed in bfloat16 or wider, within the bound.
A program may use at most 128 MiB of HBM per device.

v0:
```python
import math

import jax
import jax.numpy as jnp
from jax import lax
from jax.sharding import PartitionSpec as P

HD = 128


SQRT_HALF = 0.7071067811865476
INV_ROOT_TAU = 0.3989422804014327
NEG_LARGE = -1e30


def gelu_exact(values_in):
    return 0.5 * values_in * (1.0 + lax.erf(values_in * SQRT_HALF))


def gelu_slope(values_in):
    return (
        0.5 * (1.0 + lax.erf(values_in * SQRT_HALF))
        + values_in * jnp.exp(-0.5 * values_in * values_in) * INV_ROOT_TAU
    )


def fetch_columns(proj_weight):
    return lax.all_gather(proj_weight, "grp", axis=0, tiled=True)


def attention(queries, keys, values, lengths):
    episodes_here, tokens_here, att_width = queries.shape
    head_count = att_width // HD
    query_heads = queries.reshape(episodes_here, tokens_here, head_count, HD)
    key_heads = keys.reshape(episodes_here, tokens_here, head_count, HD)
    value_heads = values.reshape(episodes_here, tokens_here, head_count, HD)
    query_all, key_all, value_all = (
        lax.all_to_all(query_heads, "cp", split_axis=2, concat_axis=1, tiled=True),
        lax.all_to_all(key_heads, "cp", split_axis=2, concat_axis=1, tiled=True),
        lax.all_to_all(value_heads, "cp", split_axis=2, concat_axis=1, tiled=True),
    )
    seq_span = query_all.shape[1]
    scores = jnp.einsum(
        "eihd,ejhd->ehij", query_all, key_all, preferred_element_type=jnp.float32
    ) / math.sqrt(HD)
    live_keys = (jnp.arange(seq_span, dtype=jnp.int32)[None, :] < lengths[:, None])[
        :, None, None, :
    ]
    scores = jnp.where(live_keys, scores, NEG_LARGE)
    row_max = jnp.max(scores, axis=-1, keepdims=True)
    probs = jnp.where(live_keys, jnp.exp(scores - row_max), 0.0)
    row_total = jnp.sum(probs, axis=-1)
    weighted = jnp.einsum(
        "ehij,ejhd->eihd", probs.astype(jnp.bfloat16), value_all, preferred_element_type=jnp.float32
    )
    output = (weighted / jnp.transpose(row_total, (0, 2, 1))[..., None]).astype(jnp.bfloat16)
    returned = lax.all_to_all(output, "cp", split_axis=1, concat_axis=2, tiled=True)
    return returned.reshape(episodes_here, tokens_here, att_width)


def per_device(
    queries,
    keys,
    values,
    lengths,
    frame_map,
    proj_weight,
    head_weight,
    act_embed,
    actions,
    action_mask,
    group_ids,
    rewards,
):
    episodes_here, tokens_here, att_width = queries.shape
    action_count = act_embed.shape[0]
    lengths_real = lengths.astype(jnp.float32)
    attended = attention(queries, keys, values, lengths)
    proj_cols = fetch_columns(proj_weight)
    frames = jnp.dot(
        attended.reshape(episodes_here * tokens_here, att_width),
        frame_map,
        preferred_element_type=jnp.float32,
    )
    frames = frames.astype(jnp.bfloat16).reshape(episodes_here, tokens_here, frame_map.shape[1])
    all_frames = lax.all_gather(frames, "cp", axis=1, tiled=True)
    seq_span = all_frames.shape[1]
    flat_frames = all_frames.reshape(episodes_here * seq_span, all_frames.shape[2])
    col_count = proj_cols.shape[1]
    pre_act = jnp.dot(flat_frames, proj_cols, preferred_element_type=jnp.float32).reshape(
        episodes_here, seq_span, col_count
    )
    hidden = gelu_exact(pre_act)
    token_mask = (jnp.arange(seq_span, dtype=jnp.int32)[None, :] < lengths[:, None]).astype(
        jnp.float32
    )
    pooled = jnp.sum(token_mask[:, :, None] * hidden, axis=1) / lengths_real[:, None]
    sum_input = pooled[:, None, :] + act_embed[None, :, :]
    head_input = sum_input.astype(jnp.bfloat16).reshape(episodes_here * action_count, col_count)
    partial_logits = jnp.dot(head_input, head_weight, preferred_element_type=jnp.float32)
    episodes_total = episodes_here * lax.axis_size("grp")
    group_count = max(1, episodes_total // 8)
    membership = (group_ids[:, None] == jnp.arange(group_count, dtype=jnp.int32)[None, :]).astype(
        jnp.float32
    )
    masked = action_mask.astype(jnp.float32)
    logits = lax.psum(partial_logits, "cp")
    reward_sums, squares, group_sizes, mask_total = lax.psum(
        (
            jnp.sum(membership * rewards[:, None], axis=0),
            jnp.sum(membership * (rewards * rewards)[:, None], axis=0),
            jnp.sum(membership, axis=0),
            jnp.sum(masked),
        ),
        "grp",
    )
    log_all = jax.nn.log_softmax(logits, axis=-1)
    bin_ids = jnp.arange(head_weight.shape[1], dtype=jnp.int32)
    picked = (actions.reshape(-1)[:, None] == bin_ids[None, :]).astype(jnp.float32)
    logprobs = jnp.sum(picked * log_all, axis=-1).reshape(episodes_here, action_count)
    size_floor = jnp.maximum(group_sizes, 1.0)
    group_mean = reward_sums / size_floor
    variance = squares / size_floor - group_mean * group_mean
    group_scale = jnp.sqrt(jnp.maximum(variance, 1.0))
    advantage = (rewards - jnp.sum(membership * group_mean[None, :], axis=1)) / jnp.sum(
        membership * group_scale[None, :], axis=1
    )
    loss_weight = (-masked * advantage[:, None] / jnp.maximum(mask_total, 1.0)).reshape(-1)
    logit_grad = (loss_weight[:, None] * (picked - jnp.exp(log_all))).astype(jnp.bfloat16)
    head_term = lax.dot_general(
        head_input, logit_grad, (((0,), (0,)), ((), ())), preferred_element_type=jnp.float32
    )
    grad_head = lax.psum(head_term.astype(jnp.bfloat16), "grp")
    pull_back = lax.dot_general(
        logit_grad, head_weight, (((1,), (1,)), ((), ())), preferred_element_type=jnp.float32
    )
    pool_grad = jnp.sum(pull_back.reshape(episodes_here, action_count, col_count), axis=1)
    scaled_mask = token_mask / lengths_real[:, None]
    act_grad = (scaled_mask[:, :, None] * pool_grad[:, None, :] * gelu_slope(pre_act)).astype(
        jnp.bfloat16
    )
    act_flat = act_grad.reshape(episodes_here * seq_span, col_count)
    grad_proj = lax.psum_scatter(
        lax.dot_general(
            flat_frames, act_flat, (((0,), (0,)), ((), ())), preferred_element_type=jnp.float32
        ).astype(jnp.bfloat16),
        "grp",
        scatter_dimension=0,
        tiled=True,
    )
    return (logprobs, grad_proj, grad_head)


def solution(mesh):
    in_specs = (
        P("grp", "cp", None),
        P("grp", "cp", None),
        P("grp", "cp", None),
        P("grp"),
        P(),
        P("grp", "cp"),
        P("cp", None),
        P(None, "cp"),
        P("grp", None),
        P("grp", None),
        P("grp"),
        P("grp"),
    )
    out_specs = (P("grp", None), P("grp", "cp"), P("cp", None))
    return jax.shard_map(
        per_device, mesh=mesh, in_specs=in_specs, out_specs=out_specs, check_vma=False
    )
```

profile of v0, /device:TPU:0, one launch (start us, length us, event | category | flops | bytes accessed | tf_op | source)
XLA Modules:
  0.0 302.5 jit_solution(11430559681268954911)
XLA Ops:
  7.9 1.6 copy.51
  10.6 5.2 %all-to-all-start = ((bf16[2,128,16,128]{1,3,0,2:T(8,128)(2,1)}), bf16[2,128,16,128]{1,3,0,2:T(8,128)(2,1)S(1)}, u32[]{:S(2)}, u32[]{:S(2)}) async-start(bf16[2,128,16,128]{1,3,0,2:T(8,128)(2,1)} %copy.52), calls=%async_computation | async-start | bytes 2097152 | tf_op jit(solution)/shard_map/all_to_all | solution.py:38
  15.8 1.6 copy.55
  18.5 10.9 %all-to-all-done = bf16[2,128,16,128]{1,3,0,2:T(8,128)(2,1)S(1)} async-done(((bf16[2,128,16,128]{1,3,0,2:T(8,128)(2,1)}), bf16[2,128,16,128]{1,3,0,2:T(8,128)(2,1)S(1)}, u32[]{:S(2)}, u32[]{:S(2)}) %all-to-all-start) | async-done | bytes 1048608 | tf_op jit(solution)/shard_map/all_to_all | solution.py:38
  29.4 3.5 %all-to-all-start.1 = ((bf16[2,128,16,128]{1,3,0,2:T(8,128)(2,1)}), bf16[2,128,16,128]{1,3,0,2:T(8,128)(2,1)S(1)}, u32[]{:S(2)}, u32[]{:S(2)}) async-start(bf16[2,128,16,128]{1,3,0,2:T(8,128)(2,1)} %copy.56), calls=%async_computation.1 | async-start | bytes 2097152 | tf_op jit(solution)/shard_map/all_to_all | solution.py:39
  32.9 2.3 copy.59
  35.2 2.3 copy.60
  37.5 8.6 %all-to-all-done.1 = bf16[2,128,16,128]{1,3,0,2:T(8,128)(2,1)S(1)} async-done(((bf16[2,128,16,128]{1,3,0,2:T(8,128)(2,1)}), bf16[2,128,16,128]{1,3,0,2:T(8,128)(2,1)S(1)}, u32[]{:S(2)}, u32[]{:S(2)}) %all-to-all-start.1) | async-done | bytes 1048608 | tf_op jit(solution)/shard_map/all_to_all | solution.py:39
  46.2 4.3 %all-to-all-start.2 = ((bf16[2,128,16,128]{1,3,0,2:T(8,128)(2,1)}), bf16[2,128,16,128]{1,3,0,2:T(8,128)(2,1)}, u32[]{:S(2)}, u32[]{:S(2)}) async-start(bf16[2,128,16,128]{1,3,0,2:T(8,128)(2,1)} %copy.60), calls=%async_computation.2 | async-start | bytes 2097152 | tf_op jit(solution)/shard_map/all_to_all | solution.py:40
  51.9 1.4 copy.58
  53.2 10.5 %all-to-all-done.2 = bf16[2,128,16,128]{1,3,0,2:T(8,128)(2,1)} async-done(((bf16[2,128,16,128]{1,3,0,2:T(8,128)(2,1)}), bf16[2,128,16,128]{1,3,0,2:T(8,128)(2,1)}, u32[]{:S(2)}, u32[]{:S(2)}) %all-to-all-start.2) | async-done | bytes 1048608 | tf_op jit(solution)/shard_map/all_to_all | solution.py:40
  63.7 1.6 copy.62
  65.4 6.8 %fusion.33 = (f32[2,4,512]{2,1,0:T(4,128)S(1)}, bf16[2,4,512,512]{2,3,1,0:T(8,128)(2,1)}) fusion(pred[2,512]{1,0:T(4,128)(4,1)S(1)} %get-tuple-element.15, bf16[2,512,4,128]{3,1,2,0:T(8,128)(2,1)S(1)} %bitcast.54, bf16[2,512,4,128]{3,1,2,0:T(8,128)(2,1)} %bitcast.55), kind=kOutput, calls=%fused_computation.58 | convolution fusion | flops 549454336 | bytes 6308864 | tf_op jit(solution)/shard_map/sub | solution.py:51
  72.2 3.9 %fusion.16 = bf16[2,512,4,128]{3,1,2,0:T(8,128)(2,1)S(1)} fusion(bf16[2,512,4,128]{3,1,2,0:T(8,128)(2,1)S(1)} %bitcast.56, bf16[2,4,512,512]{2,3,1,0:T(8,128)(2,1)} %get-tuple-element.17, f32[2,512,4]{1,2,0:T(4,128)S(1)} %bitcast.57), kind=kOutput, calls=%fused_computation.23 | convolution fusion | flops 537919488 | bytes 6307840 | tf_op jit(solution)/shard_map/ehij,ejhd->eihd/dot_general | solution.py:53
  76.9 16.1 %all_to_all.69 = bf16[2,512,4,128]{3,2,0,1:T(4,128)(2,1)S(1)} all-to-all(bf16[2,512,4,128]{3,2,0,1:T(4,128)(2,1)S(1)} %copy.64), channel_id=1, replica_groups=mesh['cp'=4,'grp'=8] {'cp'}, dimensions={1} | all-to-all | bytes 2097152 | tf_op jit(solution)/shard_map/all_to_all | solution.py:57
  94.3 7.2 %convolution_convert_fusion = bf16[256,2176]{1,0:T(8,128)(2,1)} fusion(bf16[256,2048]{1,0:T(8,128)(2,1)S(1)} %reshape_reshape.3, bf16[2048,2176]{1,0:T(8,128)(2,1)} %param.16), kind=kOutput, calls=%fused_computation.21 | convolution fusion | flops 2282258432 | bytes 11075584 | tf_op jit(solution)/shard_map/dot_general | solution.py:80
  102.3 15.2 %all-reduce = (f32[]{:T(128)}, f32[2]{0:T(128)S(1)}, f32[2]{0:T(128)S(1)}, f32[2]{0:T(128)S(1)}) all-reduce(f32[]{:T(128)} %convert_reduce_fusion.1, f32[2]{0:T(128)S(1)} %get-tuple-element.7, f32[2]{0:T(128)S(1)} %get-tuple-element.6, f32[2]{0:T(128)S(1)} %get-tuple-element.5), channel_id=1, replica_groups=mesh['cp'=4,'grp'=8] {'grp'}, use_global_device_ids=true, to_apply=%region_16.17 | all-reduce | flops 7 | bytes 56 | tf_op jit(solution)/shard_map/psum | solution.py:108
  118.7 37.5 %all-gather.3.cloned.1.call-done = bf16[2,512,2176]{2,1,0:T(8,128)(2,1)} async-done(((bf16[2,128,2176]{2,1,0:T(8,128)(2,1)}), bf16[2,512,2176]{2,1,0:T(8,128)(2,1)}) %all-gather.3.cloned.1.call-update) | async-done | bytes 4456464 | tf_op jit(solution)/shard_map/all_gather | solution.py:86
  156.2 9.9 %multiply_reduce_fusion = (f32[2,1024]{1,0:T(2,128)S(1)}, f32[2,512,1024]{2,1,0:T(8,128)}) fusion(f32[2,512]{1,0:T(2,128)S(1)} %get-tuple-element.14, bf16[2,512,2176]{2,1,0:T(8,128)(2,1)} %all-gather.3.cloned.1.call-done, bf16[2176,1024]{1,0:T(8,128)(2,1)} %all-gather.5.cloned.1.call-done), kind=kOutput, calls=%fused_computation.14 | convolution fusion | flops 4569692160 | bytes 13119488 | tf_op jit(solution)/shard_map/dot_general | solution.py:90
  166.4 15.1 %psum.42 = f32[14,256]{1,0:T(8,128)S(1)} all-reduce(f32[14,256]{1,0:T(8,128)S(1)} %fusion.34), channel_id=1, replica_groups=mesh['cp'=4,'grp'=8] {'cp'}, use_global_device_ids=true, to_apply=%region_3.4 | all-reduce | flops 3584 | bytes 28672 | tf_op jit(solution)/shard_map/psum | solution.py:107
  183.4 10.3 %bitcast_convert_fusion = bf16[2176,1024]{1,0:T(8,128)(2,1)} fusion(bf16[2,512,2176]{2,1,0:T(8,128)(2,1)} %all-gather.3.cloned.1.call-done, f32[2,512,1024]{2,1,0:T(8,128)} %get-tuple-element.19, f32[2,1024]{1,0:T(2,128)S(1)} %reduce_sum.110, f32[2,512]{1,0:T(2,128)S(1)} %broadcast_divide_fusion.1), kind=kOutput, calls=%fused_computation.1 | convolution fusion | flops 4577165312 | bytes 13119488 | tf_op jit(solution)/shard_map/dot_general | solution.py:144
  194.5 45.4 %all-reduce.3.cloned.1.call-done = bf16[1024,256]{1,0:T(8,128)(2,1)} async-done(((bf16[1024,256]{1,0:T(8,128)(2,1)}), bf16[1024,256]{1,0:T(8,128)(2,1)}) %all-reduce.3.cloned.1.call-update) | async-done | bytes 524304 | tf_op jit(solution)/shard_map/psum | solution.py:133
  239.9 54.2 %reduce-scatter.2.cloned.1.call-done = bf16[272,1024]{1,0:T(8,128)(2,1)} async-done(((bf16[2176,1024]{1,0:T(8,128)(2,1)}), bf16[272,1024]{1,0:T(8,128)(2,1)}) %reduce-scatter.2.cloned.1.call-update) | async-done | bytes 557072 | tf_op jit(solution)/shard_map/reduce_scatter | solution.py:143
  294.1 1.9 copy.75
  (56 shorter events, 10.5 us)
Async XLA Ops:
  7.2 159.1 %copy-start = (bf16[1024,256]{1,0:T(8,128)(2,1)S(1)}, bf16[1024,256]{1,0:T(8,128)(2,1)}, u32[]{:S(2)}) copy-start(bf16[1024,256]{1,0:T(8,128)(2,1)} %param.18) | copy-start | bytes 1572868
  7.2 111.5 %all-gather.5.cloned.1.call-start = ((), (), s32[]{:S(2)}) async-start(), calls=%async_computation.6 | async-start | bytes 5013504 | tf_op jit(solution)/shard_map/all_gather | solution.py:28
  10.6 18.8 %all-to-all-start = ((bf16[2,128,16,128]{1,3,0,2:T(8,128)(2,1)}), bf16[2,128,16,128]{1,3,0,2:T(8,128)(2,1)S(1)}, u32[]{:S(2)}, u32[]{:S(2)}) async-start(bf16[2,128,16,128]{1,3,0,2:T(8,128)(2,1)} %copy.52), calls=%async_computation | async-start | bytes 2097152 | tf_op jit(solution)/shard_map/all_to_all | solution.py:38
  18.5 32.0 %copy-start.5 = (s32[2]{0:T(128)S(1)}, s32[2]{0:T(128)}, u32[]{:S(2)}) copy-start(s32[2]{0:T(128)} %param.15) | copy-start | bytes 28
  29.4 16.8 %all-to-all-start.1 = ((bf16[2,128,16,128]{1,3,0,2:T(8,128)(2,1)}), bf16[2,128,16,128]{1,3,0,2:T(8,128)(2,1)S(1)}, u32[]{:S(2)}, u32[]{:S(2)}) async-start(bf16[2,128,16,128]{1,3,0,2:T(8,128)(2,1)} %copy.56), calls=%async_computation.1 | async-start | bytes 2097152 | tf_op jit(solution)/shard_map/all_to_all | solution.py:39
  46.2 17.6 %all-to-all-start.2 = ((bf16[2,128,16,128]{1,3,0,2:T(8,128)(2,1)}), bf16[2,128,16,128]{1,3,0,2:T(8,128)(2,1)}, u32[]{:S(2)}, u32[]{:S(2)}) async-start(bf16[2,128,16,128]{1,3,0,2:T(8,128)(2,1)} %copy.60), calls=%async_computation.2 | async-start | bytes 2097152 | tf_op jit(solution)/shard_map/all_to_all | solution.py:40
  50.4 105.8 %all-gather.3.cloned.1.call-start = ((), (), s32[]{:S(2)}) async-start(), calls=%async_computation.5 | async-start | bytes 5570560 | tf_op jit(solution)/shard_map/all_gather | solution.py:86
  51.9 13.5 %copy-start.1 = (bf16[2,4,128,4,128]{4,2,1,3,0:T(8,128)(2,1)S(1)}, bf16[2,4,128,4,128]{4,2,1,3,0:T(8,128)(2,1)}, u32[]{:S(2)}) copy-start(bf16[2,4,128,4,128]{4,2,1,3,0:T(8,128)(2,1)} %copy.54) | copy-start | bytes 3145732
  94.2 7.3 %copy-start.4 = (f32[2]{0:T(128)S(1)}, f32[2]{0:T(128)}, u32[]{:S(2)}) copy-start(f32[2]{0:T(128)} %param.23) | copy-start | bytes 28
  94.2 7.4 %copy-start.6 = (s32[2,7]{1,0:T(2,128)S(1)}, s32[2,7]{1,0:T(2,128)}, u32[]{:S(2)}) copy-start(s32[2,7]{1,0:T(2,128)} %param.21) | copy-start | bytes 172
  94.2 8.0 %copy-start.3 = (s32[2]{0:T(128)S(1)}, s32[2]{0:T(128)}, u32[]{:S(2)}) copy-start(s32[2]{0:T(128)} %param.22) | copy-start | bytes 28
  94.3 23.3 %copy-start.7 = (s32[2,7]{1,0:T(2,128)S(1)}, s32[2,7]{1,0:T(2,128)}, u32[]{:S(2)}) copy-start(s32[2,7]{1,0:T(2,128)} %param.20) | copy-start | bytes 172
  101.5 138.4 %all-reduce.3.cloned.1.call-start = ((), (), s32[]{:S(2)}) async-start(), calls=%async_computation.8 | async-start | bytes 1048576 | tf_op jit(solution)/shard_map/psum | solution.py:133
  156.2 10.0 %copy-start.2 = (f32[7,1024]{1,0:T(8,128)S(1)}, f32[7,1024]{1,0:T(8,128)}, u32[]{:S(2)}) copy-start(f32[7,1024]{1,0:T(8,128)} %param.19) | copy-start | bytes 86020
  183.3 110.8 %reduce-scatter.2.cloned.1.call-start = ((), (), s32[]{:S(2)}) async-start(), calls=%async_computation.7 | async-start | bytes 5013504 | tf_op jit(solution)/shard_map/reduce_scatter | solution.py:143
Sparse Core Ops, SparseCore 0:
  9.6 51.7 all-gather.4
  101.6 54.4 all-gather.2
  183.4 56.4 all-reduce.2
  242.7 51.4 reduce-scatter.1
where the time goes:
time: 303 us
  waiting for transfers between devices  168 us (55%)
  blocking collectives  46.4 us (15%)
  matrix products  39.8 us (13%)
  local copies, waits for them, and re-layouts  19 us (6%)
  between operations  14.6 us (5%)
  starting transfers between devices  13.1 us (4%)
    reduce_scatter x1, waiting for transfers between devices, per_device(): lax.psum_scatter(lax.dot_general(flat_frames, act_flat, (((0,), (0,)), ((...  54.2 us
    psum x1, waiting for transfers between devices, per_device(): grad_head = lax.psum(head_term.astype(jnp.bfloat16), 'grp')  45.4 us
    all_gather x1, waiting for transfers between devices, per_device(): all_frames = lax.all_gather(frames, 'cp', axis=1, tiled=True)  37.5 us
    all_to_all x1, blocking collectives, attention(): lax.all_to_all(output, 'cp', split_axis=1, concat_axis=2, tiled=True)  16.1 us
    psum x1, blocking collectives, per_device(): lax.psum((jnp.sum(membership * rewards[:, None], axis=0), jnp.sum(members...  15.2 us
    psum x1, blocking collectives, per_device(): logits = lax.psum(partial_logits, 'cp')  15.1 us
    all_to_all x1, waiting for transfers between devices, attention(): lax.all_to_all(query_heads, 'cp', split_axis=2, concat_axis=1, tiled=True)  10.9 us
    all_to_all x1, waiting for transfers between devices, attention(): lax.all_to_all(value_heads, 'cp', split_axis=2, concat_axis=1, tiled=True)  10.5 us
  transfers between devices with their start and end apart: 7, of which 6 were waited for; matrix products, arithmetic and copies ran while one was open for 15% of the time, Pallas kernels for 0%

commit v1 on v0

--- a/solution.py
+++ b/solution.py
@@ -3,10 +3,12 @@
 import jax
 import jax.numpy as jnp
 from jax import lax
+from jax.experimental import pallas as pl
+from jax.experimental.pallas import tpu as pltpu
 from jax.sharding import PartitionSpec as P
 
 HD = 128
-
+ON_MESH = pl.DeviceIdType.MESH
 
 SQRT_HALF = 0.7071067811865476
 INV_ROOT_TAU = 0.3989422804014327
@@ -56,6 +58,268 @@
     output = (weighted / jnp.transpose(row_total, (0, 2, 1))[..., None]).astype(jnp.bfloat16)
     returned = lax.all_to_all(output, "cp", split_axis=1, concat_axis=2, tiled=True)
     return returned.reshape(episodes_here, tokens_here, att_width)
+
+
+def remote(source, target, send_sem, recv_sem, where):
+    return pltpu.make_async_remote_copy(
+        src_ref=source,
+        dst_ref=target,
+        send_sem=send_sem,
+        recv_sem=recv_sem,
+        device_id=where,
+        device_id_type=ON_MESH,
+    )
+
+
+def greet(peers):
+    barrier = pltpu.get_barrier_semaphore()
+    for where in peers:
+        pl.semaphore_signal(barrier, inc=1, device_id=where, device_id_type=ON_MESH)
+    pl.semaphore_wait(barrier, len(peers))
+
+
+def exchange_kernel(
+    n_cp, n_grp, logits_ref, stats_ref, logits_out, stats_out, logits_all, stats_all, sends, recvs, sends_g, recvs_g
+):
+    me, group = lax.axis_index("cp"), lax.axis_index("grp")
+    peers = [lax.rem(me + step, n_cp) for step in range(1, n_cp)]
+    peers_g = [lax.rem(group + step, n_grp) for step in range(1, n_grp)]
+    greet([(peer, group) for peer in peers] + [(me, peer) for peer in peers_g])
+    for step, peer in enumerate(peers):
+        remote(logits_ref, logits_all.at[me], sends.at[step], recvs.at[me], (peer, group)).start()
+    for step, peer in enumerate(peers_g):
+        remote(stats_ref, stats_all.at[group], sends_g.at[step], recvs_g.at[group], (me, peer)).start()
+    logits_all[me] = logits_ref[...]
+    stats_all[group] = stats_ref[...]
+    for peer in peers_g:
+        remote(stats_ref, stats_all.at[peer], sends_g.at[0], recvs_g.at[peer], (me, peer)).wait_recv()
+    stats_out[...] = jnp.sum(stats_all[...], axis=0)
+    for peer in peers:
+        remote(logits_ref, logits_all.at[peer], sends.at[0], recvs.at[peer], (peer, group)).wait_recv()
+    total = logits_all[0]
+    for slot in range(1, n_cp):
+        total = total + logits_all[slot]
+    logits_out[...] = total
+    for step, peer in enumerate(peers):
+        remote(logits_ref, logits_all.at[me], sends.at[step], recvs.at[me], (peer, group)).wait_send()
+    for step, peer in enumerate(peers_g):
+        remote(stats_ref, stats_all.at[group], sends_g.at[step], recvs_g.at[group], (me, peer)).wait_send()
+
+
+def exchange(partial_logits, stats):
+    n_cp, n_grp = lax.axis_size("cp"), lax.axis_size("grp")
+    in_vmem = pl.BlockSpec(memory_space=pltpu.VMEM)
+    dma = pltpu.SemaphoreType.DMA
+    return pl.pallas_call(
+        lambda *refs: exchange_kernel(n_cp, n_grp, *refs),
+        out_shape=(
+            jax.ShapeDtypeStruct(partial_logits.shape, jnp.float32),
+            jax.ShapeDtypeStruct(stats.shape, jnp.float32),
+        ),
+        in_specs=[in_vmem] * 2,
+        out_specs=(in_vmem,) * 2,
+        scratch_shapes=[
+            pltpu.VMEM((n_cp,) + partial_logits.shape, jnp.float32),
+            pltpu.VMEM((n_grp,) + stats.shape, jnp.float32),
+            dma((n_cp,)),
+            dma((n_cp,)),
+            dma((n_grp,)),
+            dma((n_grp,)),
+        ],
+        compiler_params=pltpu.CompilerParams(collective_id=1, has_side_effects=True),
+        name="exchange",
+    )(partial_logits, stats)
+
+
+def add_rows(target, terms):
+    rows = target.shape[0]
+    block = 16 if rows % 16 == 0 else 8
+
+    def some(index, carry):
+        at = pl.ds(pl.multiple_of(index * block, block), block)
+        total = terms[0][at, :].astype(jnp.float32)
+        for term in terms[1:]:
+            total = total + term[at, :].astype(jnp.float32)
+        target[at, :] = total.astype(target.dtype)
+        return carry
+
+    lax.fori_loop(0, rows // block, some, 0)
+
+
+def reduce_kernel(
+    n_out,
+    partial,
+    head_ref,
+    grad_ref,
+    out_ref,
+    grad_head_ref,
+    pair_recv,
+    up_send,
+    up_recv,
+    down_send,
+    down_recv,
+    head_all,
+    grad_all,
+    pair_sems,
+    up_sems,
+    down_sems,
+    head_sems,
+    grad_sems,
+):
+    n_grp = 2 * n_out
+    me, group = lax.axis_index("cp"), lax.axis_index("grp")
+    place, core = group // 2, lax.rem(group, 2)
+    sibling = (me, 2 * place + 1 - core)
+    above, below = (me, lax.rem(group + 2, n_grp)), (me, lax.rem(group + n_grp - 2, n_grp))
+    peers = [lax.rem(group + step, n_grp) for step in range(1, n_grp)]
+    greet([(me, peer) for peer in peers])
+
+    order = []
+    for step in range(n_out):
+        for target in (n_out - 1 - step, step):
+            if target not in order:
+                order.append(target)
+
+    def pair_copy(target):
+        return remote(
+            partial.at[2 * target + 1 - core],
+            pair_recv.at[target],
+            pair_sems.at[0, target],
+            pair_sems.at[1, target],
+            sibling,
+        )
+
+    def up_copy(target):
+        return remote(up_send.at[target], up_recv.at[target], up_sems.at[0, target], up_sems.at[1, target], above)
+
+    def down_copy(target):
+        return remote(
+            down_send.at[target], down_recv.at[target], down_sems.at[0, target], down_sems.at[1, target], below
+        )
+
+    for target in order:
+        pair_copy(target).start()
+
+    def head_copies(step, owner, peer):
+        return (
+            remote(head_ref, head_all.at[owner], head_sems.at[0, step], head_sems.at[1, owner], (me, peer)),
+            remote(grad_ref, grad_all.at[owner], grad_sems.at[0, step], grad_sems.at[1, owner], (me, peer)),
+        )
+
+    for step, peer in enumerate(peers):
+        for copy in head_copies(step, group, peer):
+            copy.start()
+    head_all[group] = head_ref[...]
+    grad_all[group] = grad_ref[...]
+
+    for step in range(n_out):
+        up_to, down_to = n_out - 1 - step, step
+
+        @pl.when(up_to > place)
+        def _():
+            pair_copy(up_to).wait_recv()
+            own = [partial.at[2 * up_to + core], pair_recv.at[up_to]]
+
+            @pl.when(place == 0)
+            def _():
+                add_rows(up_send.at[up_to], own)
+
+            @pl.when(place > 0)
+            def _():
+                up_copy(up_to).wait_recv()
+                add_rows(up_send.at[up_to], own + [up_recv.at[up_to]])
+
+            up_copy(up_to).start()
+
+        @pl.when(down_to < place)
+        def _():
+            pair_copy(down_to).wait_recv()
+            own = [partial.at[2 * down_to + core], pair_recv.at[down_to]]
+
+            @pl.when(place == n_out - 1)
+            def _():
+                add_rows(down_send.at[down_to], own)
+
+            @pl.when(place < n_out - 1)
+            def _():
+                down_copy(down_to).wait_recv()
+                add_rows(down_send.at[down_to], own + [down_recv.at[down_to]])
+
+            down_copy(down_to).start()
+
+    for peer in peers:
+        for copy in head_copies(0, peer, peer):
+            copy.wait_recv()
+    rows = n_grp * head_ref.shape[0]
+    grad_head_ref[...] = lax.dot_general(
+        head_all[...].reshape(rows, head_ref.shape[1]),
+        grad_all[...].reshape(rows, grad_ref.shape[1]),
+        (((0,), (0,)), ((), ())),
+        preferred_element_type=jnp.float32,
+    ).astype(jnp.bfloat16)
+
+    pair_copy(place).wait_recv()
+    own = [partial.at[group], pair_recv.at[place]]
+
+    @pl.when(place == 0)
+    def _():
+        down_copy(place).wait_recv()
+        add_rows(out_ref, own + [down_recv.at[place]])
+
+    @pl.when(place == n_out - 1)
+    def _():
+        up_copy(place).wait_recv()
+        add_rows(out_ref, own + [up_recv.at[place]])
+
+    @pl.when(jnp.logical_and(place > 0, place < n_out - 1))
+    def _():
+        up_copy(place).wait_recv()
+        down_copy(place).wait_recv()
+        add_rows(out_ref, own + [up_recv.at[place], down_recv.at[place]])
+
+    for target in range(n_out):
+        pair_copy(target).wait_send()
+
+        @pl.when(target > place)
+        def _():
+            up_copy(target).wait_send()
+
+        @pl.when(target < place)
+        def _():
+            down_copy(target).wait_send()
+
+    for step, peer in enumerate(peers):
+        for copy in head_copies(step, group, peer):
+            copy.wait_send()
+
+
+def reduce_gradients(partial, head_input, logit_grad):
+    n_grp = lax.axis_size("grp")
+    n_out = n_grp // 2
+    chunk, width = partial.shape[0] // n_grp, partial.shape[1]
+    in_vmem = pl.BlockSpec(memory_space=pltpu.VMEM)
+    dma = pltpu.SemaphoreType.DMA
+    line = pltpu.VMEM((n_out, chunk, width), jnp.bfloat16)
+    return pl.pallas_call(
+        lambda *refs: reduce_kernel(n_out, *refs),
+        out_shape=(
+            jax.ShapeDtypeStruct((chunk, width), jnp.bfloat16),
+            jax.ShapeDtypeStruct((head_input.shape[1], logit_grad.shape[1]), jnp.bfloat16),
+        ),
+        in_specs=[in_vmem] * 3,
+        out_specs=(in_vmem,) * 2,
+        scratch_shapes=[line] * 5
+        + [
+            pltpu.VMEM((n_grp,) + head_input.shape, jnp.bfloat16),
+            pltpu.VMEM((n_grp,) + logit_grad.shape, jnp.bfloat16),
+        ]
+        + [dma((2, n_out))] * 3
+        + [dma((2, n_grp))] * 2,
+        compiler_params=pltpu.CompilerParams(
+            collective_id=2, has_side_effects=True, vmem_limit_bytes=48 * 1024 * 1024
+        ),
+        name="reduce_gradients",
+    )(partial.reshape(n_grp, chunk, width), head_input, logit_grad)
 
 
 def per_device(
@@ -104,16 +368,21 @@
         jnp.float32
     )
     masked = action_mask.astype(jnp.float32)
-    logits = lax.psum(partial_logits, "cp")
-    reward_sums, squares, group_sizes, mask_total = lax.psum(
-        (
+    stats_row = jnp.concatenate(
+        [
             jnp.sum(membership * rewards[:, None], axis=0),
             jnp.sum(membership * (rewards * rewards)[:, None], axis=0),
             jnp.sum(membership, axis=0),
-            jnp.sum(masked),
-        ),
-        "grp",
-    )
+            jnp.sum(masked)[None],
+        ]
+    )
+    lanes = -(-stats_row.shape[0] // 128) * 128
+    stats_row = jnp.pad(stats_row, (0, lanes - stats_row.shape[0]))
+    logits, stats = exchange(partial_logits, jnp.broadcast_to(stats_row[None, :], (8, lanes)))
+    reward_sums = stats[0, :group_count]
+    squares = stats[0, group_count : 2 * group_count]
+    group_sizes = stats[0, 2 * group_count : 3 * group_count]
+    mask_total = stats[0, 3 * group_count]
     log_all = jax.nn.log_softmax(logits, axis=-1)
     bin_ids = jnp.arange(head_weight.shape[1], dtype=jnp.int32)
     picked = (actions.reshape(-1)[:, None] == bin_ids[None, :]).astype(jnp.float32)
@@ -127,10 +396,6 @@
     )
     loss_weight = (-masked * advantage[:, None] / jnp.maximum(mask_total, 1.0)).reshape(-1)
     logit_grad = (loss_weight[:, None] * (picked - jnp.exp(log_all))).astype(jnp.bfloat16)
-    head_term = lax.dot_general(
-        head_input, logit_grad, (((0,), (0,)), ((), ())), preferred_element_type=jnp.float32
-    )
-    grad_head = lax.psum(head_term.astype(jnp.bfloat16), "grp")
     pull_back = lax.dot_general(
         logit_grad, head_weight, (((1,), (1,)), ((), ())), preferred_element_type=jnp.float32
     )
@@ -140,13 +405,14 @@
         jnp.bfloat16
     )
     act_flat = act_grad.reshape(episodes_here * seq_span, col_count)
-    grad_proj = lax.psum_scatter(
-        lax.dot_general(
-            flat_frames, act_flat, (((0,), (0,)), ((), ())), preferred_element_type=jnp.float32
-        ).astype(jnp.bfloat16),
-        "grp",
-        scatter_dimension=0,
-        tiled=True,
+    partial_proj = lax.dot_general(
+        flat_frames, act_flat, (((0,), (0,)), ((), ())), preferred_element_type=jnp.float32
+    ).astype(jnp.bfloat16)
+    spare = -head_input.shape[0] % 16
+    grad_proj, grad_head = reduce_gradients(
+        partial_proj,
+        jnp.pad(head_input, ((0, spare), (0, 0))),
+        jnp.pad(logit_grad, ((0, spare), (0, 0))),
     )
     return (logprobs, grad_proj, grad_head)
 

time: 303 us -> 262 us (0.86)
  waiting for transfers between devices: 168 us -> 83.8 us
  Pallas kernels: 0 us -> 69 us
  blocking collectives: 46.4 us -> 16.1 us
  other arithmetic: 1.73 us -> 5.46 us
    pallas_call x0 -> x2, Pallas kernels: none -> 69 us  [the longest x1 60.7 us: reduce_gradients(): pl.pallas_call(lambda *refs: reduce_kernel(n_out, *refs), out_shape=(jax....]
    reduce_scatter x1 -> x0, waiting for transfers between devices: 54.2 us -> none  [per_device(): lax.psum_scatter(lax.dot_general(flat_frames, act_flat, (((0,), (0,)), ((...]
    psum x1 -> x0, waiting for transfers between devices: 45.4 us -> none  [per_device(): grad_head = lax.psum(head_term.astype(jnp.bfloat16), 'grp')]
    psum x2 -> x0, blocking collectives: 30.3 us -> none  [the longest x1 15.2 us: per_device(): lax.psum((jnp.sum(membership * rewards[:, None], axis=0), jnp.sum(members...]
    all_gather x1, waiting for transfers between devices: 37.5 us -> 53 us  [per_device(): all_frames = lax.all_gather(frames, 'cp', axis=1, tiled=True)]
    unnamed x20 -> x21, local copies, waits for them, and re-layouts: 7.4 us -> 7.13 us
  transfers between devices with their start and end apart: 7 -> 5, of which waited for: 6 -> 4; matrix products, arithmetic and copies ran while one was open for 15% -> 14% of each run, Pallas kernels for 0% -> 0%
where the time goes in v1:
time: 262 us; the launch traced here: 261 us
  waiting for transfers between devices  83.8 us (32%)
  Pallas kernels  69 us (26%)
  matrix products  37.8 us (14%)
  local copies, waits for them, and re-layouts  20.6 us (8%)
  blocking collectives  16.1 us (6%)
  between operations  14.9 us (6%)
  starting transfers between devices  13.1 us (5%)
  other arithmetic  5.46 us (2%)
    pallas_call x1, Pallas kernels, reduce_gradients(): pl.pallas_call(lambda *refs: reduce_kernel(n_out, *refs), out_shape=(jax....  60.7 us
    all_gather x1, waiting for transfers between devices, per_device(): all_frames = lax.all_gather(frames, 'cp', axis=1, tiled=True)  53 us
    all_to_all x1, blocking collectives, attention(): lax.all_to_all(output, 'cp', split_axis=1, concat_axis=2, tiled=True)  16.1 us
    all_to_all x1, waiting for transfers between devices, attention(): lax.all_to_all(query_heads, 'cp', split_axis=2, concat_axis=1, tiled=True)  10.9 us
    all_to_all x1, waiting for transfers between devices, attention(): lax.all_to_all(value_heads, 'cp', split_axis=2, concat_axis=1, tiled=True)  10.5 us
    dot_general x1, matrix products, per_device(): jnp.dot(flat_frames, proj_cols, preferred_element_type=jnp.float32)  9.92 us
    dot_general x1, matrix products, per_device(): lax.dot_general(flat_frames, act_flat, (((0,), (0,)), ((), ())), preferre...  8.88 us
    all_to_all x1, waiting for transfers between devices, attention(): lax.all_to_all(key_heads, 'cp', split_axis=2, concat_axis=1, tiled=True)  8.65 us
  transfers between devices with their start and end apart: 5, of which 4 were waited for; matrix products, arithmetic and copies ran while one was open for 14% of the time, Pallas kernels for 0%

profile of v1, /device:TPU:0, one launch (start us, length us, event | category | flops | bytes accessed | tf_op | source)
XLA Modules:
  0.0 260.7 jit_solution(6042986328923627714)
XLA Ops:
  7.9 1.6 copy.51
  10.6 5.2 %all-to-all-start = ((bf16[2,128,16,128]{1,3,0,2:T(8,128)(2,1)}), bf16[2,128,16,128]{1,3,0,2:T(8,128)(2,1)S(1)}, u32[]{:S(2)}, u32[]{:S(2)}) async-start(bf16[2,128,16,128]{1,3,0,2:T(8,128)(2,1)} %copy.52), calls=%async_computation | async-start | bytes 2097152 | tf_op jit(solution)/shard_map/all_to_all | solution.py:40
  15.8 1.6 copy.55
  17.4 1.1 copy.56
  18.5 10.9 %all-to-all-done = bf16[2,128,16,128]{1,3,0,2:T(8,128)(2,1)S(1)} async-done(((bf16[2,128,16,128]{1,3,0,2:T(8,128)(2,1)}), bf16[2,128,16,128]{1,3,0,2:T(8,128)(2,1)S(1)}, u32[]{:S(2)}, u32[]{:S(2)}) %all-to-all-start) | async-done | bytes 1048608 | tf_op jit(solution)/shard_map/all_to_all | solution.py:40
  29.4 3.5 %all-to-all-start.1 = ((bf16[2,128,16,128]{1,3,0,2:T(8,128)(2,1)}), bf16[2,128,16,128]{1,3,0,2:T(8,128)(2,1)S(1)}, u32[]{:S(2)}, u32[]{:S(2)}) async-start(bf16[2,128,16,128]{1,3,0,2:T(8,128)(2,1)} %copy.56), calls=%async_computation.1 | async-start | bytes 2097152 | tf_op jit(solution)/shard_map/all_to_all | solution.py:41
  32.9 2.3 copy.59
  35.2 2.3 copy.60
  37.5 8.6 %all-to-all-done.1 = bf16[2,128,16,128]{1,3,0,2:T(8,128)(2,1)S(1)} async-done(((bf16[2,128,16,128]{1,3,0,2:T(8,128)(2,1)}), bf16[2,128,16,128]{1,3,0,2:T(8,128)(2,1)S(1)}, u32[]{:S(2)}, u32[]{:S(2)}) %all-to-all-start.1) | async-done | bytes 1048608 | tf_op jit(solution)/shard_map/all_to_all | solution.py:41
  46.2 4.3 %all-to-all-start.2 = ((bf16[2,128,16,128]{1,3,0,2:T(8,128)(2,1)}), bf16[2,128,16,128]{1,3,0,2:T(8,128)(2,1)}, u32[]{:S(2)}, u32[]{:S(2)}) async-start(bf16[2,128,16,128]{1,3,0,2:T(8,128)(2,1)} %copy.60), calls=%async_computation.2 | async-start | bytes 2097152 | tf_op jit(solution)/shard_map/all_to_all | solution.py:42
  50.6 1.3 copy.54
  51.9 1.4 copy.58
  53.2 10.5 %all-to-all-done.2 = bf16[2,128,16,128]{1,3,0,2:T(8,128)(2,1)} async-done(((bf16[2,128,16,128]{1,3,0,2:T(8,128)(2,1)}), bf16[2,128,16,128]{1,3,0,2:T(8,128)(2,1)}, u32[]{:S(2)}, u32[]{:S(2)}) %all-to-all-start.2) | async-done | bytes 1048608 | tf_op jit(solution)/shard_map/all_to_all | solution.py:42
  63.7 1.6 copy.62
  65.4 6.8 %fusion.32 = (f32[2,4,512]{2,1,0:T(4,128)S(1)}, bf16[2,4,512,512]{2,3,1,0:T(8,128)(2,1)}) fusion(pred[2,512]{1,0:T(4,128)(4,1)S(1)} %get-tuple-element.21, bf16[2,512,4,128]{3,1,2,0:T(8,128)(2,1)S(1)} %bitcast.61, bf16[2,512,4,128]{3,1,2,0:T(8,128)(2,1)} %bitcast.62), kind=kOutput, calls=%fused_computation.61 | convolution fusion | flops 549454336 | bytes 6308864 | tf_op jit(solution)/shard_map/sub | solution.py:53
  72.2 3.9 %fusion.16 = bf16[2,512,4,128]{3,1,2,0:T(8,128)(2,1)S(1)} fusion(bf16[2,512,4,128]{3,1,2,0:T(8,128)(2,1)S(1)} %bitcast.63, bf16[2,4,512,512]{2,3,1,0:T(8,128)(2,1)} %get-tuple-element.23, f32[2,512,4]{1,2,0:T(4,128)S(1)} %bitcast.65), kind=kOutput, calls=%fused_computation.23 | convolution fusion | flops 537919488 | bytes 6307840 | tf_op jit(solution)/shard_map/ehij,ejhd->eihd/dot_general | solution.py:55
  77.0 16.1 %all_to_all.69 = bf16[2,512,4,128]{3,2,0,1:T(4,128)(2,1)S(1)} all-to-all(bf16[2,512,4,128]{3,2,0,1:T(4,128)(2,1)S(1)} %copy.64), channel_id=1, replica_groups=mesh['cp'=4,'grp'=8] {'cp'}, dimensions={1} | all-to-all | bytes 2097152 | tf_op jit(solution)/shard_map/all_to_all | solution.py:59
  94.3 7.2 %convolution_convert_fusion = bf16[256,2176]{1,0:T(8,128)(2,1)} fusion(bf16[256,2048]{1,0:T(8,128)(2,1)S(1)} %reshape_reshape.3, bf16[2048,2176]{1,0:T(8,128)(2,1)} %param.16), kind=kOutput, calls=%fused_computation.21 | convolution fusion | flops 2282258432 | bytes 11075584 | tf_op jit(solution)/shard_map/dot_general | solution.py:344
  103.1 53.0 %all-gather.3.cloned.1.call-done = bf16[2,512,2176]{2,1,0:T(8,128)(2,1)} async-done(((bf16[2,128,2176]{2,1,0:T(8,128)(2,1)}), bf16[2,512,2176]{2,1,0:T(8,128)(2,1)}) %all-gather.3.cloned.1.call-update) | async-done | bytes 4456464 | tf_op jit(solution)/shard_map/all_gather | solution.py:350
  156.2 9.9 %multiply_reduce_fusion = (f32[2,1024]{1,0:T(2,128)S(1)}, f32[2,512,1024]{2,1,0:T(8,128)}) fusion(f32[2,512]{1,0:T(2,128)S(1)} %get-tuple-element.20, bf16[2,512,2176]{2,1,0:T(8,128)(2,1)} %all-gather.3.cloned.1.call-done, bf16[2176,1024]{1,0:T(8,128)(2,1)} %all-gather.5.cloned.1.call-done), kind=kOutput, calls=%fused_computation.14 | convolution fusion | flops 4569692160 | bytes 13119488 | tf_op jit(solution)/shard_map/dot_general | solution.py:354
  167.6 8.3 %exchange.1 = (f32[14,256]{1,0:T(8,128)}, f32[8,128]{1,0:T(8,128)}) custom-call(f32[14,256]{1,0:T(8,128)} %fusion.33.refs_0_, f32[8,128]{1,0:T(8,128)} %broadcast_in_dim.28.refs_1_), custom_call_target="tpu_custom_call" | custom-call | tf_op jit(solution)/shard_map/exchange/pallas_call | solution.py:113
  176.7 1.3 slice.15
  182.0 8.9 %bitcast_convert_fusion = bf16[2176,1024]{1,0:T(8,128)(2,1)S(1)} fusion(bf16[2,512,2176]{2,1,0:T(8,128)(2,1)} %all-gather.3.cloned.1.call-done, f32[2,512,1024]{2,1,0:T(8,128)} %get-tuple-element.25, f32[2,1024]{1,0:T(2,128)S(1)} %reduce_sum.110, f32[2,512]{1,0:T(2,128)S(1)} %broadcast_divide_fusion.1), kind=kOutput, calls=%fused_computation.1 | convolution fusion | flops 4577165312 | bytes 13119488 | tf_op jit(solution)/shard_map/dot_general | solution.py:408
  190.9 60.7 %reduce_gradients.1 = (bf16[272,1024]{1,0:T(8,128)(2,1)S(1)}, bf16[1024,256]{1,0:T(8,128)(2,1)S(1)}) custom-call(bf16[8,272,1024]{2,1,0:T(8,128)(2,1)S(1)} %bitcast.52, bf16[16,1024]{1,0:T(8,128)(2,1)S(1)} %pad.13.refs_1_, bf16[16,256]{1,0:T(8,128)(2,1)S(1)} %pad.14.refs_2_), custom_call_target="tpu_custom_call" | custom-call | tf_op jit(solution)/shard_map/reduce_gradients/pallas_call | solution.py:303
  (55 shorter events, 13.4 us)
Async XLA Ops:
  7.2 159.1 %copy-start = (bf16[1024,256]{1,0:T(8,128)(2,1)S(1)}, bf16[1024,256]{1,0:T(8,128)(2,1)}, u32[]{:S(2)}) copy-start(bf16[1024,256]{1,0:T(8,128)(2,1)} %param.18) | copy-start | bytes 1572868
  7.2 96.0 %all-gather.5.cloned.1.call-start = ((), (), s32[]{:S(2)}) async-start(), calls=%async_computation.5 | async-start | bytes 5013504 | tf_op jit(solution)/shard_map/all_gather | solution.py:30
  10.6 18.8 %all-to-all-start = ((bf16[2,128,16,128]{1,3,0,2:T(8,128)(2,1)}), bf16[2,128,16,128]{1,3,0,2:T(8,128)(2,1)S(1)}, u32[]{:S(2)}, u32[]{:S(2)}) async-start(bf16[2,128,16,128]{1,3,0,2:T(8,128)(2,1)} %copy.52), calls=%async_computation | async-start | bytes 2097152 | tf_op jit(solution)/shard_map/all_to_all | solution.py:40
  18.5 32.0 %copy-start.4 = (s32[2]{0:T(128)S(1)}, s32[2]{0:T(128)}, u32[]{:S(2)}) copy-start(s32[2]{0:T(128)} %param.15) | copy-start | bytes 28
  29.4 16.8 %all-to-all-start.1 = ((bf16[2,128,16,128]{1,3,0,2:T(8,128)(2,1)}), bf16[2,128,16,128]{1,3,0,2:T(8,128)(2,1)S(1)}, u32[]{:S(2)}, u32[]{:S(2)}) async-start(bf16[2,128,16,128]{1,3,0,2:T(8,128)(2,1)} %copy.56), calls=%async_computation.1 | async-start | bytes 2097152 | tf_op jit(solution)/shard_map/all_to_all | solution.py:41
  46.2 17.6 %all-to-all-start.2 = ((bf16[2,128,16,128]{1,3,0,2:T(8,128)(2,1)}), bf16[2,128,16,128]{1,3,0,2:T(8,128)(2,1)}, u32[]{:S(2)}, u32[]{:S(2)}) async-start(bf16[2,128,16,128]{1,3,0,2:T(8,128)(2,1)} %copy.60), calls=%async_computation.2 | async-start | bytes 2097152 | tf_op jit(solution)/shard_map/all_to_all | solution.py:42
  50.4 105.8 %all-gather.3.cloned.1.call-start = ((), (), s32[]{:S(2)}) async-start(), calls=%async_computation.4 | async-start | bytes 5570560 | tf_op jit(solution)/shard_map/all_gather | solution.py:350
  51.9 13.5 %copy-start.1 = (bf16[2,4,128,4,128]{4,2,1,3,0:T(8,128)(2,1)S(1)}, bf16[2,4,128,4,128]{4,2,1,3,0:T(8,128)(2,1)}, u32[]{:S(2)}) copy-start(bf16[2,4,128,4,128]{4,2,1,3,0:T(8,128)(2,1)} %copy.54) | copy-start | bytes 3145732
  94.2 7.3 %copy-start.5 = (f32[2]{0:T(128)S(1)}, f32[2]{0:T(128)}, u32[]{:S(2)}) copy-start(f32[2]{0:T(128)} %param.23) | copy-start | bytes 28
  94.2 7.3 %copy-start.7 = (s32[2,7]{1,0:T(2,128)S(1)}, s32[2,7]{1,0:T(2,128)}, u32[]{:S(2)}) copy-start(s32[2,7]{1,0:T(2,128)} %param.20) | copy-start | bytes 172
  94.2 7.4 %copy-start.6 = (s32[2,7]{1,0:T(2,128)S(1)}, s32[2,7]{1,0:T(2,128)}, u32[]{:S(2)}) copy-start(s32[2,7]{1,0:T(2,128)} %param.21) | copy-start | bytes 172
  94.3 8.0 %copy-start.3 = (s32[2]{0:T(128)S(1)}, s32[2]{0:T(128)}, u32[]{:S(2)}) copy-start(s32[2]{0:T(128)} %param.22) | copy-start | bytes 28
  156.2 10.0 %copy-start.2 = (f32[7,1024]{1,0:T(8,128)S(1)}, f32[7,1024]{1,0:T(8,128)}, u32[]{:S(2)}) copy-start(f32[7,1024]{1,0:T(8,128)} %param.19) | copy-start | bytes 86020
Sparse Core Ops, SparseCore 0:
  9.6 51.7 all-gather.4
  101.6 54.4 all-gather.2

commit v2 on v1

--- a/solution.py
+++ b/solution.py
@@ -24,40 +24,6 @@
         0.5 * (1.0 + lax.erf(values_in * SQRT_HALF))
         + values_in * jnp.exp(-0.5 * values_in * values_in) * INV_ROOT_TAU
     )
-
-
-def fetch_columns(proj_weight):
-    return lax.all_gather(proj_weight, "grp", axis=0, tiled=True)
-
-
-def attention(queries, keys, values, lengths):
-    episodes_here, tokens_here, att_width = queries.shape
-    head_count = att_width // HD
-    query_heads = queries.reshape(episodes_here, tokens_here, head_count, HD)
-    key_heads = keys.reshape(episodes_here, tokens_here, head_count, HD)
-    value_heads = values.reshape(episodes_here, tokens_here, head_count, HD)
-    query_all, key_all, value_all = (
-        lax.all_to_all(query_heads, "cp", split_axis=2, concat_axis=1, tiled=True),
-        lax.all_to_all(key_heads, "cp", split_axis=2, concat_axis=1, tiled=True),
-        lax.all_to_all(value_heads, "cp", split_axis=2, concat_axis=1, tiled=True),
-    )
-    seq_span = query_all.shape[1]
-    scores = jnp.einsum(
-        "eihd,ejhd->ehij", query_all, key_all, preferred_element_type=jnp.float32
-    ) / math.sqrt(HD)
-    live_keys = (jnp.arange(seq_span, dtype=jnp.int32)[None, :] < lengths[:, None])[
-        :, None, None, :
-    ]
-    scores = jnp.where(live_keys, scores, NEG_LARGE)
-    row_max = jnp.max(scores, axis=-1, keepdims=True)
-    probs = jnp.where(live_keys, jnp.exp(scores - row_max), 0.0)
-    row_total = jnp.sum(probs, axis=-1)
-    weighted = jnp.einsum(
-        "ehij,ejhd->eihd", probs.astype(jnp.bfloat16), value_all, preferred_element_type=jnp.float32
-    )
-    output = (weighted / jnp.transpose(row_total, (0, 2, 1))[..., None]).astype(jnp.bfloat16)
-    returned = lax.all_to_all(output, "cp", split_axis=1, concat_axis=2, tiled=True)
-    return returned.reshape(episodes_here, tokens_here, att_width)
 
 
 def remote(source, target, send_sem, recv_sem, where):
@@ -322,6 +288,256 @@
     )(partial.reshape(n_grp, chunk, width), head_input, logit_grad)
 
 
+def front_kernel(
+    n_cp,
+    n_out,
+    length_ref,
+    query_ref,
+    key_ref,
+    value_ref,
+    map_ref,
+    shard_ref,
+    frames_ref,
+    columns_ref,
+    heads_all,
+    blocks,
+    map_held,
+    total,
+    local_sems,
+    swap_send,
+    swap_recv,
+    block_send,
+    block_recv,
+    shard_send,
+    shard_recv,
+    pass_send,
+    pass_recv,
+):
+    episodes, tokens, _ = query_ref.shape
+    width = blocks.shape[2]
+    seq = tokens * n_cp
+    n_grp = 2 * n_out
+    me, group = lax.axis_index("cp"), lax.axis_index("grp")
+    place, core = group // 2, lax.rem(group, 2)
+    sibling = 2 * place + 1 - core
+    square = n_cp == 4
+    if square:
+        row_peer = me + 1 - 2 * lax.rem(me, 2)
+        col_peer = lax.rem(me + 2, 4)
+        far_peer = lax.rem(row_peer + 2, 4)
+        peers = [far_peer, row_peer, col_peer]
+    else:
+        peers = [lax.rem(me + step, n_cp) for step in range(1, n_cp)]
+    lines = [2 * lax.rem(place + step, n_out) + core for step in range(1, n_out)]
+
+    map_copy = pltpu.make_async_copy(map_ref, map_held, local_sems.at[0])
+    map_copy.start()
+    keep_copy = pltpu.make_async_copy(shard_ref, columns_ref.at[group], local_sems.at[1])
+    keep_copy.start()
+
+    def my_copy(tensor, source, episode):
+        return pltpu.make_async_copy(
+            source.at[episode, :, pl.ds(pl.multiple_of(me * width, 128), width)],
+            heads_all.at[tensor, episode, pl.ds(pl.multiple_of(me * tokens, 8), tokens), :],
+            local_sems.at[2 + tensor * episodes + episode],
+        )
+
+    def swap_copy(tensor, source, episode, step, owner, peer):
+        return remote(
+            source.at[episode, :, pl.ds(pl.multiple_of(peer * width, 128), width)],
+            heads_all.at[tensor, episode, pl.ds(pl.multiple_of(owner * tokens, 8), tokens), :],
+            swap_send.at[tensor, episode, step],
+            swap_recv.at[tensor, episode, owner],
+            (peer, group),
+        )
+
+    sources = (query_ref, key_ref, value_ref)
+    for episode in range(episodes):
+        for tensor, source in enumerate(sources):
+            my_copy(tensor, source, episode).start()
+    greet([(peer, group) for peer in peers] + [(me, peer) for peer in lines] + [(me, sibling)])
+    for episode in range(episodes):
+        for tensor, source in enumerate(sources):
+            for step, peer in enumerate(peers):
+                swap_copy(tensor, source, episode, step, me, peer).start()
+
+    def shard_copy(step, owner, peer):
+        return remote(shard_ref, columns_ref.at[owner], shard_send.at[step], shard_recv.at[owner], (me, peer))
+
+    def pass_copy(step, owner, source):
+        return remote(source, columns_ref.at[owner], pass_send.at[step], pass_recv.at[owner], (me, sibling))
+
+    for step, peer in reversed(list(enumerate(lines))):
+        shard_copy(step, group, peer).start()
+    pass_copy(n_out - 1, group, shard_ref).start()
+
+    def rows_of(owner, episode, first, count):
+        return blocks.at[owner, pl.ds(episode * seq + first, count), :]
+
+    def block_copy(episode, step, owner, peer, first, count, part):
+        return remote(
+            rows_of(owner, episode, first, count),
+            rows_of(owner, episode, first, count),
+            block_send.at[episode, step],
+            block_recv.at[episode, owner, part],
+            (peer, group),
+        )
+
+    strip = min(seq, 256)
+
+    def attend(episode):
+        live = lax.broadcasted_iota(jnp.int32, (strip, seq), 1) < length_ref[episode]
+
+        def one_head(head, carry):
+            at = pl.ds(pl.multiple_of(head * HD, HD), HD)
+            key_head = heads_all[1, episode, :, at]
+            value_head = heads_all[2, episode, :, at]
+            for first in range(0, seq, strip):
+                query_head = heads_all[0, episode, first : first + strip, at]
+                scores = lax.dot_general(
+                    query_head, key_head, (((1,), (1,)), ((), ())), preferred_element_type=jnp.float32
+                )
+                scores = jnp.where(live, scores * (1.0 / math.sqrt(HD)), NEG_LARGE)
+                probs = jnp.exp(scores - jnp.max(scores, axis=1, keepdims=True))
+                row_total = jnp.sum(probs, axis=1, keepdims=True)
+                weighted = jnp.dot(probs.astype(jnp.bfloat16), value_head, preferred_element_type=jnp.float32)
+                blocks[me, episode * seq + first : episode * seq + first + strip, at] = (
+                    weighted / row_total
+                ).astype(jnp.bfloat16)
+            return carry
+
+        lax.fori_loop(0, width // HD, one_head, 0)
+
+    def add_frames(episode, owner, opens, closes):
+        tall = min(seq, 512)
+        whole, spare = divmod(frames_ref.shape[2], 256)
+        depth = pl.ds(pl.multiple_of(owner * width, 128), width)
+
+        def one_tile(first, at):
+            rows = pl.ds(episode * seq + first, tall)
+            part = jnp.dot(blocks[owner, rows, :], map_held[depth, at], preferred_element_type=jnp.float32)
+            if not opens:
+                part = part + total[rows, at]
+            if closes:
+                frames_ref[episode, first : first + tall, at] = part.astype(jnp.bfloat16)
+            else:
+                total[rows, at] = part
+
+        for first in range(0, seq, tall):
+
+            def step(index, carry):
+                one_tile(first, pl.ds(pl.multiple_of(index * 256, 256), 256))
+                return carry
+
+            lax.fori_loop(0, whole, step, 0)
+            if spare:
+                one_tile(first, pl.ds(whole * 256, spare))
+
+    for episode in range(episodes):
+        for tensor, source in enumerate(sources):
+            my_copy(tensor, source, episode).wait()
+            for peer in peers:
+                swap_copy(tensor, source, episode, 0, peer, peer).wait_recv()
+        attend(episode)
+        if square:
+            block_copy(episode, 0, me, row_peer, 0, seq, 0).start()
+            block_copy(episode, 1, me, col_peer, 0, seq, 0).start()
+        else:
+            for step, peer in enumerate(peers):
+                block_copy(episode, step, me, peer, 0, seq, 0).start()
+        if episode == 0:
+            map_copy.wait()
+        add_frames(episode, me, True, False)
+
+    def forward_shards():
+        for step, peer in enumerate(lines):
+            shard_copy(step, peer, peer).wait_recv()
+            pass_copy(step, peer, columns_ref.at[peer]).start()
+
+    half = seq // 2
+    if square:
+        for episode in range(episodes):
+            block_copy(episode, 0, row_peer, row_peer, 0, seq, 0).wait_recv()
+            block_copy(episode, 2, row_peer, col_peer, 0, half, 0).start()
+            block_copy(episode, 1, col_peer, col_peer, 0, seq, 0).wait_recv()
+            block_copy(episode, 3, col_peer, row_peer, half, half, 1).start()
+            add_frames(episode, row_peer, False, False)
+            add_frames(episode, col_peer, False, False)
+        forward_shards()
+        for episode in range(episodes):
+            block_copy(episode, 2, far_peer, col_peer, 0, half, 0).wait_recv()
+            block_copy(episode, 3, far_peer, row_peer, half, half, 1).wait_recv()
+            add_frames(episode, far_peer, False, True)
+    else:
+        for episode in range(episodes):
+            for step, peer in enumerate(peers):
+                block_copy(episode, step, peer, peer, 0, seq, 0).wait_recv()
+                add_frames(episode, peer, False, step == len(peers) - 1)
+        forward_shards()
+
+    for step, peer in enumerate(lines):
+        pass_copy(step, peer + 1 - 2 * core, columns_ref.at[peer]).wait_recv()
+    pass_copy(n_out - 1, sibling, shard_ref).wait_recv()
+    keep_copy.wait()
+    for episode in range(episodes):
+        for tensor, source in enumerate(sources):
+            for step, peer in enumerate(peers):
+                swap_copy(tensor, source, episode, step, me, peer).wait_send()
+        if square:
+            block_copy(episode, 0, me, row_peer, 0, seq, 0).wait_send()
+            block_copy(episode, 1, me, col_peer, 0, seq, 0).wait_send()
+            block_copy(episode, 2, row_peer, col_peer, 0, half, 0).wait_send()
+            block_copy(episode, 3, col_peer, row_peer, half, half, 1).wait_send()
+        else:
+            for step, peer in enumerate(peers):
+                block_copy(episode, step, me, peer, 0, seq, 0).wait_send()
+    for step, peer in enumerate(lines):
+        shard_copy(step, group, peer).wait_send()
+        pass_copy(step, peer, columns_ref.at[peer]).wait_send()
+    pass_copy(n_out - 1, group, shard_ref).wait_send()
+
+
+def front(queries, keys, values, lengths, frame_map, proj_weight):
+    n_cp, n_grp = lax.axis_size("cp"), lax.axis_size("grp")
+    n_out = n_grp // 2
+    episodes, tokens, att_width = queries.shape
+    seq, width = tokens * n_cp, att_width // n_cp
+    chunk, cols = proj_weight.shape
+    features = frame_map.shape[1]
+    anywhere = pl.BlockSpec(memory_space=pl.ANY)
+    in_vmem = pl.BlockSpec(memory_space=pltpu.VMEM)
+    dma = pltpu.SemaphoreType.DMA
+    frames, columns = pl.pallas_call(
+        lambda *refs: front_kernel(n_cp, n_out, *refs),
+        out_shape=(
+            jax.ShapeDtypeStruct((episodes, seq, features), jnp.bfloat16),
+            jax.ShapeDtypeStruct((n_grp, chunk, cols), jnp.bfloat16),
+        ),
+        in_specs=[pl.BlockSpec(memory_space=pltpu.SMEM)] + [anywhere] * 4 + [in_vmem],
+        out_specs=(in_vmem, anywhere),
+        scratch_shapes=[
+            pltpu.VMEM((3, episodes, seq, width), jnp.bfloat16),
+            pltpu.VMEM((n_cp, episodes * seq, width), jnp.bfloat16),
+            pltpu.VMEM(frame_map.shape, jnp.bfloat16),
+            pltpu.VMEM((episodes * seq, features), jnp.float32),
+            dma((2 + 3 * episodes,)),
+            dma((3, episodes, n_cp)),
+            dma((3, episodes, n_cp)),
+            dma((episodes, max(n_cp, 4))),
+            dma((episodes, n_cp, 2)),
+            dma((n_out,)),
+            dma((n_grp,)),
+            dma((n_out,)),
+            dma((n_grp,)),
+        ],
+        compiler_params=pltpu.CompilerParams(
+            collective_id=3, has_side_effects=True, vmem_limit_bytes=60 * 1024 * 1024
+        ),
+        name="front",
+    )(lengths, queries, keys, values, frame_map, proj_weight)
+    return frames, columns.reshape(n_grp * chunk, cols)
+
+
 def per_device(
     queries,
     keys,
@@ -339,15 +555,7 @@
     episodes_here, tokens_here, att_width = queries.shape
     action_count = act_embed.shape[0]
     lengths_real = lengths.astype(jnp.float32)
-    attended = attention(queries, keys, values, lengths)
-    proj_cols = fetch_columns(proj_weight)
-    frames = jnp.dot(
-        attended.reshape(episodes_here * tokens_here, att_width),
-        frame_map,
-        preferred_element_type=jnp.float32,
-    )
-    frames = frames.astype(jnp.bfloat16).reshape(episodes_here, tokens_here, frame_map.shape[1])
-    all_frames = lax.all_gather(frames, "cp", axis=1, tiled=True)
+    all_frames, proj_cols = front(queries, keys, values, lengths, frame_map, proj_weight)
     seq_span = all_frames.shape[1]
     flat_frames = all_frames.reshape(episodes_here * seq_span, all_frames.shape[2])
     col_count = proj_cols.shape[1]

time: 262 us -> 181 us (0.69)
  waiting for transfers between devices: 83.8 us -> 0 us
  Pallas kernels: 69 us -> 149 us
  matrix products: 37.8 us -> 19.9 us
  local copies, waits for them, and re-layouts: 20.6 us -> 4.37 us
  blocking collectives: 16.1 us -> 0 us
  between operations: 14.9 us -> 1.45 us
  starting transfers between devices: 13.1 us -> 0 us
    pallas_call x0 -> x1, Pallas kernels: none -> 81.6 us  [front(): pl.pallas_call(lambda *refs: front_kernel(n_cp, n_out, *refs), out_shape=...]
    all_gather x2 -> x0, waiting for transfers between devices: 53 us -> none  [the longest x1 53 us: per_device(): all_frames = lax.all_gather(frames, 'cp', axis=1, tiled=True)]
    all_to_all x3 -> x0, waiting for transfers between devices: 30.1 us -> none  [the longest x1 10.9 us: attention(): lax.all_to_all(query_heads, 'cp', split_axis=2, concat_axis=1, tiled=True)]
    all_to_all x1 -> x0, blocking collectives: 16.1 us -> none  [attention(): lax.all_to_all(output, 'cp', split_axis=1, concat_axis=2, tiled=True)]
    all_to_all x3 -> x0, starting transfers between devices: 13 us -> none  [the longest x1 5.19 us: attention(): lax.all_to_all(query_heads, 'cp', split_axis=2, concat_axis=1, tiled=True)]
    dot_general x2 -> x0, matrix products: 11.1 us -> none  [the longest x1 7.22 us: per_device(): jnp.dot(attended.reshape(episodes_here * tokens_here, att_width), frame_m...]
    sub x1 -> x0, matrix products: 6.84 us -> none  [attention(): probs = jnp.where(live_keys, jnp.exp(scores - row_max), 0.0)]
    unnamed x21 -> x16, local copies, waits for them, and re-layouts: 7.13 us -> 1.63 us
  transfers between devices with their start and end apart: 5 -> 0, of which waited for: 4 -> 0; matrix products, arithmetic and copies ran while one was open for 14% -> 0% of each run, Pallas kernels for 0% -> 0%
where the time goes in v2:
time: 181 us; the launch traced here: 180 us
  Pallas kernels  149 us (82%)
  matrix products  19.9 us (11%)
  other arithmetic  5.46 us (3%)
  local copies, waits for them, and re-layouts  4.37 us (2%)
    pallas_call x1, Pallas kernels, front(): pl.pallas_call(lambda *refs: front_kernel(n_cp, n_out, *refs), out_shape=...  81.6 us
    pallas_call x1, Pallas kernels, reduce_gradients(): pl.pallas_call(lambda *refs: reduce_kernel(n_out, *refs), out_shape=(jax....  60.3 us
    dot_general x1, matrix products, per_device(): jnp.dot(flat_frames, proj_cols, preferred_element_type=jnp.float32)  9.97 us
    dot_general x1, matrix products, per_device(): lax.dot_general(flat_frames, act_flat, (((0,), (0,)), ((), ())), preferre...  8.86 us
    pallas_call x1, Pallas kernels, exchange(): pl.pallas_call(lambda *refs: exchange_kernel(n_cp, n_grp, *refs), out_sha...  6.98 us

profile of v2, /device:TPU:0, one launch (start us, length us, event | category | flops | bytes accessed | tf_op | source)
XLA Modules:
  0.0 180.0 jit_solution(8391604692002248664)
XLA Ops:
  0.7 81.6 %front.1 = (bf16[2,512,2176]{2,1,0:T(8,128)(2,1)}, bf16[8,272,1024]{2,1,0:T(8,128)(2,1)}) custom-call(s32[2]{0:T(128)} %refs_0_.1, bf16[2,128,2048]{2,1,0:T(8,128)(2,1)} %refs_1_.1, bf16[2,128,2048]{2,1,0:T(8,128)(2,1)} %refs_2_.1, bf16[2,128,2048]{2,1,0:T(8,128)(2,1)} %refs_3_.1, bf16[2048,2176]{1,0:T(8,128)(2,1)} %refs_4_.1, bf16[272,1024]{1,0:T(8,128)(2,1)} %refs_5_.1), custom_call_target="tpu_custom_call" | custom-call | tf_op jit(solution)/shard_map/front/pallas_call | solution.py:510
  82.3 10.0 %multiply_reduce_fusion = (f32[2,1024]{1,0:T(2,128)S(1)}, f32[2,512,1024]{2,1,0:T(8,128)}) fusion(f32[2,512]{1,0:T(2,128)S(1)} %compare_convert_fusion, bf16[2,512,2176]{2,1,0:T(8,128)(2,1)} %get-tuple-element.9, bf16[2176,1024,1]{1,0,2:T(8,128)(2,1)} %bitcast.20), kind=kOutput, calls=%fused_computation.8 | convolution fusion | flops 4569692160 | bytes 13119488 | tf_op jit(solution)/shard_map/dot_general | solution.py:562
  92.3 0.1 broadcast_divide_fusion
  92.4 0.8 fusion.15.refs_0_
  93.2 0.1 select_reduce_fusion.4
  93.3 0.6 convert_reduce_fusion
  93.9 0.7 select_maximum_fusion
  94.7 0.6 broadcast_in_dim.7.refs_1_
  95.3 7.0 %exchange.1 = (f32[14,256]{1,0:T(8,128)}, f32[8,128]{1,0:T(8,128)}) custom-call(f32[14,256]{1,0:T(8,128)} %fusion.15.refs_0_, f32[8,128]{1,0:T(8,128)} %broadcast_in_dim.7.refs_1_), custom_call_target="tpu_custom_call" | custom-call | tf_op jit(solution)/shard_map/exchange/pallas_call | solution.py:79
  102.3 0.9 sqrt_bitcast_fusion
  103.1 0.2 select_reduce_fusion.2
  103.3 1.3 slice.15
  105.3 0.1 mul.140
  105.4 0.8 reduce_max.10
  106.2 0.9 exponential_reduce_fusion
  107.2 0.1 eq.28
  107.2 0.9 multiply_convert_fusion
  108.2 0.2 fusion.16
  108.5 0.1 broadcast_divide_fusion.1
  108.5 8.9 %bitcast_convert_fusion = bf16[2176,1024]{1,0:T(8,128)(2,1)S(1)} fusion(bf16[2,512,2176]{2,1,0:T(8,128)(2,1)} %get-tuple-element.9, f32[2,512,1024]{2,1,0:T(8,128)} %get-tuple-element.25, f32[2,1024]{1,0:T(2,128)S(1)} %reduce_sum.100, f32[2,512]{1,0:T(2,128)S(1)} %broadcast_divide_fusion.1), kind=kOutput, calls=%fused_computation | convolution fusion | flops 4577165312 | bytes 13119488 | tf_op jit(solution)/shard_map/dot_general | solution.py:616
  117.4 60.3 %reduce_gradients.1 = (bf16[272,1024]{1,0:T(8,128)(2,1)S(1)}, bf16[1024,256]{1,0:T(8,128)(2,1)S(1)}) custom-call(bf16[8,272,1024]{2,1,0:T(8,128)(2,1)S(1)} %bitcast.18, bf16[16,1024]{1,0:T(8,128)(2,1)S(1)} %pad.13.refs_1_, bf16[16,256]{1,0:T(8,128)(2,1)S(1)} %pad.14.refs_2_), custom_call_target="tpu_custom_call" | custom-call | tf_op jit(solution)/shard_map/reduce_gradients/pallas_call | solution.py:269
  177.7 0.6 reshape.112
  178.4 0.8 copy.21
  179.2 0.8 copy.22
  (26 shorter events, 0.3 us)
Async XLA Ops:
  0.6 91.8 %copy-start = (bf16[1024,256]{1,0:T(8,128)(2,1)S(1)}, bf16[1024,256]{1,0:T(8,128)(2,1)}, u32[]{:S(2)}) copy-start(bf16[1024,256]{1,0:T(8,128)(2,1)} %param.18) | copy-start | bytes 1572868
  0.6 81.6 %copy-start.2 = (s32[2]{0:T(128)S(1)}, s32[2]{0:T(128)}, u32[]{:S(2)}) copy-start(s32[2]{0:T(128)} %refs_0_.1) | copy-start | bytes 28
  82.3 10.1 %copy-start.1 = (f32[7,1024]{1,0:T(8,128)S(1)}, f32[7,1024]{1,0:T(8,128)}, u32[]{:S(2)}) copy-start(f32[7,1024]{1,0:T(8,128)} %param.19) | copy-start | bytes 86020
  82.3 10.9 %copy-start.4 = (f32[2]{0:T(128)S(1)}, f32[2]{0:T(128)}, u32[]{:S(2)}) copy-start(f32[2]{0:T(128)} %param.23) | copy-start | bytes 28
  82.3 10.9 %copy-start.3 = (s32[2]{0:T(128)S(1)}, s32[2]{0:T(128)}, u32[]{:S(2)}) copy-start(s32[2]{0:T(128)} %param.22) | copy-start | bytes 28
  82.3 11.0 %copy-start.5 = (s32[2,7]{1,0:T(2,128)S(1)}, s32[2,7]{1,0:T(2,128)}, u32[]{:S(2)}) copy-start(s32[2,7]{1,0:T(2,128)} %param.21) | copy-start | bytes 172
  82.3 24.8 %copy-start.6 = (s32[2,7]{1,0:T(2,128)S(1)}, s32[2,7]{1,0:T(2,128)}, u32[]{:S(2)}) copy-start(s32[2,7]{1,0:T(2,128)} %param.20) | copy-start | bytes 172

commit v3 on v2

--- a/solution.py
+++ b/solution.py
@@ -44,248 +44,336 @@
     pl.semaphore_wait(barrier, len(peers))
 
 
-def exchange_kernel(
-    n_cp, n_grp, logits_ref, stats_ref, logits_out, stats_out, logits_all, stats_all, sends, recvs, sends_g, recvs_g
-):
-    me, group = lax.axis_index("cp"), lax.axis_index("grp")
-    peers = [lax.rem(me + step, n_cp) for step in range(1, n_cp)]
-    peers_g = [lax.rem(group + step, n_grp) for step in range(1, n_grp)]
-    greet([(peer, group) for peer in peers] + [(me, peer) for peer in peers_g])
-    for step, peer in enumerate(peers):
-        remote(logits_ref, logits_all.at[me], sends.at[step], recvs.at[me], (peer, group)).start()
-    for step, peer in enumerate(peers_g):
-        remote(stats_ref, stats_all.at[group], sends_g.at[step], recvs_g.at[group], (me, peer)).start()
-    logits_all[me] = logits_ref[...]
-    stats_all[group] = stats_ref[...]
-    for peer in peers_g:
-        remote(stats_ref, stats_all.at[peer], sends_g.at[0], recvs_g.at[peer], (me, peer)).wait_recv()
-    stats_out[...] = jnp.sum(stats_all[...], axis=0)
-    for peer in peers:
-        remote(logits_ref, logits_all.at[peer], sends.at[0], recvs.at[peer], (peer, group)).wait_recv()
-    total = logits_all[0]
-    for slot in range(1, n_cp):
-        total = total + logits_all[slot]
-    logits_out[...] = total
-    for step, peer in enumerate(peers):
-        remote(logits_ref, logits_all.at[me], sends.at[step], recvs.at[me], (peer, group)).wait_send()
-    for step, peer in enumerate(peers_g):
-        remote(stats_ref, stats_all.at[group], sends_g.at[step], recvs_g.at[group], (me, peer)).wait_send()
-
-
-def exchange(partial_logits, stats):
-    n_cp, n_grp = lax.axis_size("cp"), lax.axis_size("grp")
-    in_vmem = pl.BlockSpec(memory_space=pltpu.VMEM)
-    dma = pltpu.SemaphoreType.DMA
-    return pl.pallas_call(
-        lambda *refs: exchange_kernel(n_cp, n_grp, *refs),
-        out_shape=(
-            jax.ShapeDtypeStruct(partial_logits.shape, jnp.float32),
-            jax.ShapeDtypeStruct(stats.shape, jnp.float32),
-        ),
-        in_specs=[in_vmem] * 2,
-        out_specs=(in_vmem,) * 2,
-        scratch_shapes=[
-            pltpu.VMEM((n_cp,) + partial_logits.shape, jnp.float32),
-            pltpu.VMEM((n_grp,) + stats.shape, jnp.float32),
-            dma((n_cp,)),
-            dma((n_cp,)),
-            dma((n_grp,)),
-            dma((n_grp,)),
-        ],
-        compiler_params=pltpu.CompilerParams(collective_id=1, has_side_effects=True),
-        name="exchange",
-    )(partial_logits, stats)
-
-
-def add_rows(target, terms):
-    rows = target.shape[0]
-    block = 16 if rows % 16 == 0 else 8
-
-    def some(index, carry):
-        at = pl.ds(pl.multiple_of(index * block, block), block)
-        total = terms[0][at, :].astype(jnp.float32)
-        for term in terms[1:]:
-            total = total + term[at, :].astype(jnp.float32)
-        target[at, :] = total.astype(target.dtype)
-        return carry
-
-    lax.fori_loop(0, rows // block, some, 0)
-
-
-def reduce_kernel(
+def tail_kernel(
+    n_cp,
     n_out,
-    partial,
+    group_count,
+    action_ref,
+    mask_ref,
+    id_ref,
+    reward_ref,
+    frames_ref,
+    slope_ref,
     head_ref,
-    grad_ref,
+    weight_ref,
+    logprob_ref,
     out_ref,
     grad_head_ref,
+    logits_send,
+    logits_all,
+    stats_send,
+    stats_all,
+    head_all,
+    grad_send,
+    grad_all,
+    pulls,
+    moments,
+    pair_send,
     pair_recv,
     up_send,
     up_recv,
     down_send,
     down_recv,
-    head_all,
-    grad_all,
+    logits_sems,
+    stats_sems,
+    head_sems,
+    grad_sems,
     pair_sems,
     up_sems,
     down_sems,
-    head_sems,
-    grad_sems,
 ):
+    episodes, action_count = action_ref.shape
+    rows, _ = head_ref.shape
+    bins = weight_ref.shape[1]
+    seq = frames_ref.shape[1]
+    chunk, width = out_ref.shape
+    parts, span = pair_send.shape[1], pair_send.shape[3]
     n_grp = 2 * n_out
     me, group = lax.axis_index("cp"), lax.axis_index("grp")
     place, core = group // 2, lax.rem(group, 2)
     sibling = (me, 2 * place + 1 - core)
     above, below = (me, lax.rem(group + 2, n_grp)), (me, lax.rem(group + n_grp - 2, n_grp))
-    peers = [lax.rem(group + step, n_grp) for step in range(1, n_grp)]
-    greet([(me, peer) for peer in peers])
-
-    order = []
-    for step in range(n_out):
-        for target in (n_out - 1 - step, step):
-            if target not in order:
-                order.append(target)
-
-    def pair_copy(target):
+    peers = [lax.rem(me + step, n_cp) for step in range(1, n_cp)]
+    peers_g = [lax.rem(group + step, n_grp) for step in range(1, n_grp)]
+
+    def to_all(send, everyone, sems, step, owner, where):
+        return remote(send, everyone.at[owner], sems.at[0, step], sems.at[1, owner], where)
+
+    lane = lax.broadcasted_iota(jnp.int32, (8, 128), 1)
+    stats = jnp.zeros((8, 128), jnp.float32)
+    for episode in range(episodes):
+        reward, member = reward_ref[episode], id_ref[episode]
+        stats = stats + jnp.where(lane == member, reward, 0.0)
+        stats = stats + jnp.where(lane == group_count + member, reward * reward, 0.0)
+        stats = stats + jnp.where(lane == 2 * group_count + member, 1.0, 0.0)
+        for action in range(action_count):
+            valid = mask_ref[episode, action].astype(jnp.float32)
+            stats = stats + jnp.where(lane == 3 * group_count, valid, 0.0)
+    stats_send[...] = stats
+    stats_all[group] = stats
+    partial = jnp.dot(head_ref[...], weight_ref[...], preferred_element_type=jnp.float32)
+    logits_send[...] = partial
+    logits_all[me] = partial
+    head_all[group] = head_ref[...]
+
+    greet([(peer, group) for peer in peers] + [(me, peer) for peer in peers_g])
+    for step, peer in enumerate(peers):
+        to_all(logits_send, logits_all, logits_sems, step, me, (peer, group)).start()
+    for step, peer in enumerate(peers_g):
+        to_all(stats_send, stats_all, stats_sems, step, group, (me, peer)).start()
+    for step, peer in enumerate(peers_g):
+        to_all(head_ref, head_all, head_sems, step, group, (me, peer)).start()
+
+    features = frames_ref.shape[2]
+    whole, spare = divmod(features, 256)
+
+    def moment(episode, at, down):
+        moments[episode, down, :] = lax.dot_general(
+            frames_ref[episode, :, at],
+            slope_ref[episode],
+            (((0,), (0,)), ((), ())),
+            preferred_element_type=jnp.float32,
+        )
+
+    for episode in range(episodes):
+
+        def one_tile(index, carry):
+            at = pl.ds(pl.multiple_of(index * 256, 256), 256)
+            moment(episode, at, at)
+            return carry
+
+        lax.fori_loop(0, whole, one_tile, 0)
+        if spare:
+            moment(episode, pl.ds(whole * 256, spare), pl.ds(whole * 256, spare))
+
+    for peer in peers:
+        to_all(logits_send, logits_all, logits_sems, 0, peer, (peer, group)).wait_recv()
+    logits = logits_all[0]
+    for slot in range(1, n_cp):
+        logits = logits + logits_all[slot]
+    for peer in peers_g:
+        to_all(stats_send, stats_all, stats_sems, 0, peer, (me, peer)).wait_recv()
+    stats = jnp.sum(stats_all[...], axis=0)[0:1]
+    lane = lane[0:1]
+
+    def entry(index):
+        return jnp.sum(jnp.where(lane == index, stats, 0.0), axis=1, keepdims=True)
+
+    mask_total = jnp.maximum(entry(3 * group_count), 1.0)
+    row = lax.broadcasted_iota(jnp.int32, (rows, 1), 0)
+    chosen = jnp.zeros((rows, 1), jnp.int32)
+    loss_weight = jnp.zeros((rows, 1), jnp.float32)
+    for episode in range(episodes):
+        member = id_ref[episode]
+        size = jnp.maximum(entry(2 * group_count + member), 1.0)
+        mean = entry(member) / size
+        variance = entry(group_count + member) / size - mean * mean
+        advantage = (reward_ref[episode] - mean) / jnp.sqrt(jnp.maximum(variance, 1.0))
+        for action in range(action_count):
+            here = row == episode * action_count + action
+            chosen = jnp.where(here, action_ref[episode, action], chosen)
+            valid = mask_ref[episode, action].astype(jnp.float32)
+            loss_weight = jnp.where(here, -valid * advantage / mask_total, loss_weight)
+    shifted = logits - jnp.max(logits, axis=1, keepdims=True)
+    log_all = shifted - jnp.log(jnp.sum(jnp.exp(shifted), axis=1, keepdims=True))
+    picked = (lax.broadcasted_iota(jnp.int32, (rows, bins), 1) == chosen).astype(jnp.float32)
+    logprob = jnp.sum(picked * log_all, axis=1, keepdims=True)
+    logit_grad = (loss_weight * (picked - jnp.exp(log_all))).astype(jnp.bfloat16)
+    pull_back = lax.dot_general(
+        logit_grad, weight_ref[...], (((1,), (1,)), ((), ())), preferred_element_type=jnp.float32
+    )
+    for episode in range(episodes):
+        mine = jnp.logical_and(row >= episode * action_count, row < (episode + 1) * action_count)
+        pulls[episode : episode + 1, :] = jnp.sum(jnp.where(mine, pull_back, 0.0), axis=0, keepdims=True)
+    grad_send[...] = logit_grad
+    grad_all[group] = logit_grad
+
+    block = 16 if chunk % 16 == 0 else 8
+
+    def fill(target, slot, part, terms):
+        at = pl.ds(part * span, span)
+        scales = [pulls[episode : episode + 1, at] for episode in range(episodes)]
+
+        def some(index, carry):
+            here = pl.ds(pl.multiple_of(index * block, block), block)
+            down = pl.ds(pl.multiple_of(slot * chunk + index * block, 8), block)
+            total = moments[0, down, at] * scales[0]
+            for episode in range(1, episodes):
+                total = total + moments[episode, down, at] * scales[episode]
+            for term in terms:
+                total = total + term[here, :].astype(jnp.float32)
+            target[here, :] = total.astype(jnp.bfloat16)
+            return carry
+
+        lax.fori_loop(0, chunk // block, some, 0)
+
+    def hop(send, recv, sems, target, part, where):
         return remote(
-            partial.at[2 * target + 1 - core],
-            pair_recv.at[target],
-            pair_sems.at[0, target],
-            pair_sems.at[1, target],
-            sibling,
+            send.at[target, part],
+            recv.at[target, part],
+            sems.at[0, target, part],
+            sems.at[1, target, part],
+            where,
         )
 
-    def up_copy(target):
-        return remote(up_send.at[target], up_recv.at[target], up_sems.at[0, target], up_sems.at[1, target], above)
-
-    def down_copy(target):
-        return remote(
-            down_send.at[target], down_recv.at[target], down_sems.at[0, target], down_sems.at[1, target], below
-        )
-
-    for target in order:
-        pair_copy(target).start()
-
-    def head_copies(step, owner, peer):
-        return (
-            remote(head_ref, head_all.at[owner], head_sems.at[0, step], head_sems.at[1, owner], (me, peer)),
-            remote(grad_ref, grad_all.at[owner], grad_sems.at[0, step], grad_sems.at[1, owner], (me, peer)),
-        )
-
-    for step, peer in enumerate(peers):
-        for copy in head_copies(step, group, peer):
-            copy.start()
-    head_all[group] = head_ref[...]
-    grad_all[group] = grad_ref[...]
-
-    for step in range(n_out):
-        up_to, down_to = n_out - 1 - step, step
-
-        @pl.when(up_to > place)
+    def pair_copy(target, part):
+        return hop(pair_send, pair_recv, pair_sems, target, part, sibling)
+
+    def up_copy(target, part):
+        return hop(up_send, up_recv, up_sems, target, part, above)
+
+    def down_copy(target, part):
+        return hop(down_send, down_recv, down_sems, target, part, below)
+
+    def give(target):
+        for part in range(parts):
+            fill(pair_send.at[target, part], 2 * target + 1 - core, part, [])
+            pair_copy(target, part).start()
+
+    last = n_out - 1
+    for time in range(last):
+        rising, falling = last + place - time, time - last + place
+
+        @pl.when(time >= place)
         def _():
-            pair_copy(up_to).wait_recv()
-            own = [partial.at[2 * up_to + core], pair_recv.at[up_to]]
-
-            @pl.when(place == 0)
+            give(rising)
+
+        @pl.when(time >= last - place)
+        def _():
+            give(falling)
+
+    give(place)
+
+    for step, peer in enumerate(peers_g):
+        to_all(grad_send, grad_all, grad_sems, step, group, (me, peer)).start()
+
+    def pass_on(target, part, send, recv, copy):
+        pair_copy(target, part).wait_recv()
+        own = [pair_recv.at[target, part]]
+        ends = place == 0 if copy is up_copy else place == last
+
+        @pl.when(ends)
+        def _():
+            fill(send.at[target, part], 2 * target + core, part, own)
+
+        @pl.when(jnp.logical_not(ends))
+        def _():
+            copy(target, part).wait_recv()
+            fill(send.at[target, part], 2 * target + core, part, own + [recv.at[target, part]])
+
+        copy(target, part).start()
+
+    for time in range(last):
+        rising, falling = last + place - time, time - last + place
+        for part in range(parts):
+
+            @pl.when(time >= place)
             def _():
-                add_rows(up_send.at[up_to], own)
-
-            @pl.when(place > 0)
+                pass_on(rising, part, up_send, up_recv, up_copy)
+
+            @pl.when(time >= last - place)
             def _():
-                up_copy(up_to).wait_recv()
-                add_rows(up_send.at[up_to], own + [up_recv.at[up_to]])
-
-            up_copy(up_to).start()
-
-        @pl.when(down_to < place)
-        def _():
-            pair_copy(down_to).wait_recv()
-            own = [partial.at[2 * down_to + core], pair_recv.at[down_to]]
-
-            @pl.when(place == n_out - 1)
-            def _():
-                add_rows(down_send.at[down_to], own)
-
-            @pl.when(place < n_out - 1)
-            def _():
-                down_copy(down_to).wait_recv()
-                add_rows(down_send.at[down_to], own + [down_recv.at[down_to]])
-
-            down_copy(down_to).start()
-
-    for peer in peers:
-        for copy in head_copies(0, peer, peer):
-            copy.wait_recv()
-    rows = n_grp * head_ref.shape[0]
+                pass_on(falling, part, down_send, down_recv, down_copy)
+
+    cell = lax.broadcasted_iota(jnp.int32, (episodes, action_count), 0) * action_count
+    cell = cell + lax.broadcasted_iota(jnp.int32, (episodes, action_count), 1)
+    laid = jnp.zeros((episodes, action_count), jnp.float32)
+    for index in range(episodes * action_count):
+        laid = jnp.where(cell == index, logprob[index : index + 1, :], laid)
+    logprob_ref[...] = laid
+    for peer in peers_g:
+        to_all(head_ref, head_all, head_sems, 0, peer, (me, peer)).wait_recv()
+        to_all(grad_send, grad_all, grad_sems, 0, peer, (me, peer)).wait_recv()
     grad_head_ref[...] = lax.dot_general(
-        head_all[...].reshape(rows, head_ref.shape[1]),
-        grad_all[...].reshape(rows, grad_ref.shape[1]),
+        head_all[...].reshape(n_grp * rows, width),
+        grad_all[...].reshape(n_grp * rows, bins),
         (((0,), (0,)), ((), ())),
         preferred_element_type=jnp.float32,
     ).astype(jnp.bfloat16)
 
-    pair_copy(place).wait_recv()
-    own = [partial.at[group], pair_recv.at[place]]
-
-    @pl.when(place == 0)
-    def _():
-        down_copy(place).wait_recv()
-        add_rows(out_ref, own + [down_recv.at[place]])
-
-    @pl.when(place == n_out - 1)
-    def _():
-        up_copy(place).wait_recv()
-        add_rows(out_ref, own + [up_recv.at[place]])
-
-    @pl.when(jnp.logical_and(place > 0, place < n_out - 1))
-    def _():
-        up_copy(place).wait_recv()
-        down_copy(place).wait_recv()
-        add_rows(out_ref, own + [up_recv.at[place], down_recv.at[place]])
+    for part in range(parts):
+        goal = out_ref.at[:, pl.ds(part * span, span)]
+        pair_copy(place, part).wait_recv()
+        own = [pair_recv.at[place, part]]
+        rose, fell = up_recv.at[place, part], down_recv.at[place, part]
+
+        @pl.when(place == 0)
+        def _():
+            down_copy(place, part).wait_recv()
+            fill(goal, group, part, own + [fell])
+
+        @pl.when(place == last)
+        def _():
+            up_copy(place, part).wait_recv()
+            fill(goal, group, part, own + [rose])
+
+        @pl.when(jnp.logical_and(place > 0, place < last))
+        def _():
+            up_copy(place, part).wait_recv()
+            down_copy(place, part).wait_recv()
+            fill(goal, group, part, own + [rose, fell])
 
     for target in range(n_out):
-        pair_copy(target).wait_send()
-
-        @pl.when(target > place)
-        def _():
-            up_copy(target).wait_send()
-
-        @pl.when(target < place)
-        def _():
-            down_copy(target).wait_send()
+        for part in range(parts):
+            pair_copy(target, part).wait_send()
+
+            @pl.when(target > place)
+            def _():
+                up_copy(target, part).wait_send()
+
+            @pl.when(target < place)
+            def _():
+                down_copy(target, part).wait_send()
 
     for step, peer in enumerate(peers):
-        for copy in head_copies(step, group, peer):
-            copy.wait_send()
-
-
-def reduce_gradients(partial, head_input, logit_grad):
-    n_grp = lax.axis_size("grp")
+        to_all(logits_send, logits_all, logits_sems, step, me, (peer, group)).wait_send()
+    for step, peer in enumerate(peers_g):
+        to_all(stats_send, stats_all, stats_sems, step, group, (me, peer)).wait_send()
+        to_all(head_ref, head_all, head_sems, step, group, (me, peer)).wait_send()
+        to_all(grad_send, grad_all, grad_sems, step, group, (me, peer)).wait_send()
+
+
+def tail(actions, action_mask, group_ids, rewards, frames, slopes, head_input, head_weight):
+    n_cp, n_grp = lax.axis_size("cp"), lax.axis_size("grp")
     n_out = n_grp // 2
-    chunk, width = partial.shape[0] // n_grp, partial.shape[1]
+    episodes = actions.shape[0]
+    group_count = max(1, episodes * n_grp // 8)
+    features, width = frames.shape[2], slopes.shape[2]
+    rows, bins = head_input.shape[0], head_weight.shape[1]
+    chunk, parts = features // n_grp, 2
+    in_smem = pl.BlockSpec(memory_space=pltpu.SMEM)
     in_vmem = pl.BlockSpec(memory_space=pltpu.VMEM)
     dma = pltpu.SemaphoreType.DMA
-    line = pltpu.VMEM((n_out, chunk, width), jnp.bfloat16)
+    line = pltpu.VMEM((n_out, parts, chunk, width // parts), jnp.bfloat16)
     return pl.pallas_call(
-        lambda *refs: reduce_kernel(n_out, *refs),
+        lambda *refs: tail_kernel(n_cp, n_out, group_count, *refs),
         out_shape=(
+            jax.ShapeDtypeStruct(actions.shape, jnp.float32),
             jax.ShapeDtypeStruct((chunk, width), jnp.bfloat16),
-            jax.ShapeDtypeStruct((head_input.shape[1], logit_grad.shape[1]), jnp.bfloat16),
+            jax.ShapeDtypeStruct((width, bins), jnp.bfloat16),
         ),
-        in_specs=[in_vmem] * 3,
-        out_specs=(in_vmem,) * 2,
-        scratch_shapes=[line] * 5
-        + [
-            pltpu.VMEM((n_grp,) + head_input.shape, jnp.bfloat16),
-            pltpu.VMEM((n_grp,) + logit_grad.shape, jnp.bfloat16),
+        in_specs=[in_smem] * 4 + [in_vmem] * 4,
+        out_specs=(in_vmem,) * 3,
+        scratch_shapes=[
+            pltpu.VMEM((rows, bins), jnp.float32),
+            pltpu.VMEM((n_cp, rows, bins), jnp.float32),
+            pltpu.VMEM((8, 128), jnp.float32),
+            pltpu.VMEM((n_grp, 8, 128), jnp.float32),
+            pltpu.VMEM((n_grp, rows, width), jnp.bfloat16),
+            pltpu.VMEM((rows, bins), jnp.bfloat16),
+            pltpu.VMEM((n_grp, rows, bins), jnp.bfloat16),
+            pltpu.VMEM((-(-episodes // 8) * 8, width), jnp.float32),
+            pltpu.VMEM((episodes, features, width), jnp.float32),
         ]
-        + [dma((2, n_out))] * 3
-        + [dma((2, n_grp))] * 2,
+        + [line] * 6
+        + [dma((2, n_cp))]
+        + [dma((2, n_grp))] * 3
+        + [dma((2, n_out, parts))] * 3,
         compiler_params=pltpu.CompilerParams(
-            collective_id=2, has_side_effects=True, vmem_limit_bytes=48 * 1024 * 1024
+            collective_id=1, has_side_effects=True, vmem_limit_bytes=60 * 1024 * 1024
         ),
-        name="reduce_gradients",
-    )(partial.reshape(n_grp, chunk, width), head_input, logit_grad)
+        name="tail",
+    )(actions, action_mask, group_ids, rewards, frames, slopes, head_input, head_weight)
 
 
 def front_kernel(
@@ -569,58 +657,18 @@
     pooled = jnp.sum(token_mask[:, :, None] * hidden, axis=1) / lengths_real[:, None]
     sum_input = pooled[:, None, :] + act_embed[None, :, :]
     head_input = sum_input.astype(jnp.bfloat16).reshape(episodes_here * action_count, col_count)
-    partial_logits = jnp.dot(head_input, head_weight, preferred_element_type=jnp.float32)
-    episodes_total = episodes_here * lax.axis_size("grp")
-    group_count = max(1, episodes_total // 8)
-    membership = (group_ids[:, None] == jnp.arange(group_count, dtype=jnp.int32)[None, :]).astype(
-        jnp.float32
-    )
-    masked = action_mask.astype(jnp.float32)
-    stats_row = jnp.concatenate(
-        [
-            jnp.sum(membership * rewards[:, None], axis=0),
-            jnp.sum(membership * (rewards * rewards)[:, None], axis=0),
-            jnp.sum(membership, axis=0),
-            jnp.sum(masked)[None],
-        ]
-    )
-    lanes = -(-stats_row.shape[0] // 128) * 128
-    stats_row = jnp.pad(stats_row, (0, lanes - stats_row.shape[0]))
-    logits, stats = exchange(partial_logits, jnp.broadcast_to(stats_row[None, :], (8, lanes)))
-    reward_sums = stats[0, :group_count]
-    squares = stats[0, group_count : 2 * group_count]
-    group_sizes = stats[0, 2 * group_count : 3 * group_count]
-    mask_total = stats[0, 3 * group_count]
-    log_all = jax.nn.log_softmax(logits, axis=-1)
-    bin_ids = jnp.arange(head_weight.shape[1], dtype=jnp.int32)
-    picked = (actions.reshape(-1)[:, None] == bin_ids[None, :]).astype(jnp.float32)
-    logprobs = jnp.sum(picked * log_all, axis=-1).reshape(episodes_here, action_count)
-    size_floor = jnp.maximum(group_sizes, 1.0)
-    group_mean = reward_sums / size_floor
-    variance = squares / size_floor - group_mean * group_mean
-    group_scale = jnp.sqrt(jnp.maximum(variance, 1.0))
-    advantage = (rewards - jnp.sum(membership * group_mean[None, :], axis=1)) / jnp.sum(
-        membership * group_scale[None, :], axis=1
-    )
-    loss_weight = (-masked * advantage[:, None] / jnp.maximum(mask_total, 1.0)).reshape(-1)
-    logit_grad = (loss_weight[:, None] * (picked - jnp.exp(log_all))).astype(jnp.bfloat16)
-    pull_back = lax.dot_general(
-        logit_grad, head_weight, (((1,), (1,)), ((), ())), preferred_element_type=jnp.float32
-    )
-    pool_grad = jnp.sum(pull_back.reshape(episodes_here, action_count, col_count), axis=1)
+    spare = -head_input.shape[0] % 16
     scaled_mask = token_mask / lengths_real[:, None]
-    act_grad = (scaled_mask[:, :, None] * pool_grad[:, None, :] * gelu_slope(pre_act)).astype(
-        jnp.bfloat16
-    )
-    act_flat = act_grad.reshape(episodes_here * seq_span, col_count)
-    partial_proj = lax.dot_general(
-        flat_frames, act_flat, (((0,), (0,)), ((), ())), preferred_element_type=jnp.float32
-    ).astype(jnp.bfloat16)
-    spare = -head_input.shape[0] % 16
-    grad_proj, grad_head = reduce_gradients(
-        partial_proj,
+    slopes = (scaled_mask[:, :, None] * gelu_slope(pre_act)).astype(jnp.bfloat16)
+    logprobs, grad_proj, grad_head = tail(
+        actions,
+        action_mask,
+        group_ids,
+        rewards,
+        all_frames,
+        slopes,
         jnp.pad(head_input, ((0, spare), (0, 0))),
-        jnp.pad(logit_grad, ((0, spare), (0, 0))),
+        head_weight,
     )
     return (logprobs, grad_proj, grad_head)
 

time: 181 us -> 155 us (0.86)
  Pallas kernels: 149 us -> 136 us
  matrix products: 19.9 us -> 11 us
  other arithmetic: 5.46 us -> 2.2 us
    pallas_call x2 -> x1, Pallas kernels: 67.3 us -> 54.2 us  [tail(): pl.pallas_call(lambda *refs: tail_kernel(n_cp, n_out, group_count, *refs)...]
    dot_general x3 -> x0, matrix products: 9.89 us -> none  [the longest x1 8.86 us: per_device(): lax.dot_general(flat_frames, act_flat, (((0,), (0,)), ((), ())), preferre...]
    unnamed x16 -> x5, local copies, waits for them, and re-layouts: 1.63 us -> 5 us
where the time goes in v3:
time: 155 us
  Pallas kernels  136 us (88%)
  matrix products  11 us (7%)
  local copies, waits for them, and re-layouts  5.64 us (4%)
  other arithmetic  2.2 us (1%)
    pallas_call x1, Pallas kernels, front(): pl.pallas_call(lambda *refs: front_kernel(n_cp, n_out, *refs), out_shape=...  81.5 us
    pallas_call x1, Pallas kernels, tail(): pl.pallas_call(lambda *refs: tail_kernel(n_cp, n_out, group_count, *refs)...  54.2 us
    dot_general x1, matrix products, per_device(): jnp.dot(flat_frames, proj_cols, preferred_element_type=jnp.float32)  11 us
    unnamed x5, local copies, waits for them, and re-layouts  5 us

profile of v3, /device:TPU:0, one launch (start us, length us, event | category | flops | bytes accessed | tf_op | source)
XLA Modules:
  0.0 155.1 jit_solution(18203592406996246558)
XLA Ops:
  0.6 0.7 convert_element_type.26
  1.3 0.7 broadcast_divide_fusion.1
  2.0 0.7 compare_convert_fusion
  2.7 81.5 %front.1 = (bf16[2,512,2176]{2,1,0:T(8,128)(2,1)}, bf16[8,272,1024]{2,1,0:T(8,128)(2,1)}) custom-call(s32[2]{0:T(128)} %refs_0_.2, bf16[2,128,2048]{2,1,0:T(8,128)(2,1)} %refs_1_.2, bf16[2,128,2048]{2,1,0:T(8,128)(2,1)} %refs_2_.2, bf16[2,128,2048]{2,1,0:T(8,128)(2,1)} %refs_3_.2, bf16[2048,2176]{1,0:T(8,128)(2,1)} %refs_4_.1, bf16[272,1024]{1,0:T(8,128)(2,1)} %refs_5_.1), custom_call_target="tpu_custom_call" | custom-call | tf_op jit(solution)/shard_map/front/pallas_call | solution.py:598
  84.2 0.0 copy-start
  84.2 11.0 %multiply_reduce_fusion = (f32[2,1024]{1,0:T(2,128)S(1)}, bf16[2,512,1024]{2,1,0:T(8,128)(2,1)}) fusion(f32[2,512]{1,0:T(2,128)S(1)} %compare_convert_fusion, f32[2,512]{1,0:T(2,128)S(1)} %broadcast_divide_fusion.1, bf16[2,512,2176]{2,1,0:T(8,128)(2,1)} %get-tuple-element.5.refs_4_, bf16[2176,1024,1]{1,0,2:T(8,128)(2,1)} %bitcast.5), kind=kOutput, calls=%fused_computation.7 | convolution fusion | flops 4578080768 | bytes 11026432 | tf_op jit(solution)/shard_map/dot_general | solution.py:650
  95.2 0.1 broadcast_divide_fusion
  95.3 0.0 copy-done
  95.3 0.6 pad.4.refs_6_
  96.0 54.2 %tail.1 = (f32[2,7]{1,0:T(2,128)}, bf16[272,1024]{1,0:T(8,128)(2,1)}, bf16[1024,256]{1,0:T(8,128)(2,1)}) custom-call(s32[2,7]{1,0:T(2,128)} %refs_0_.3, s32[2,7]{1,0:T(2,128)} %refs_1_.3, s32[2]{0:T(128)} %refs_2_.3, f32[2]{0:T(128)} %refs_3_.3, bf16[2,512,2176]{2,1,0:T(8,128)(2,1)} %get-tuple-element.5.refs_4_, ...), custom_call_target="tpu_custom_call" | custom-call | tf_op jit(solution)/shard_map/tail/pallas_call | solution.py:348
  150.1 1.2 copy.18
  151.4 1.9 %copy.19 = bf16[272,1024]{1,0:T(8,128)(2,1)} copy(bf16[272,1024]{1,0:T(8,128)(2,1)} %get-tuple-element.13) | data formatting | bytes 1114112
  153.2 1.9 %copy.20 = bf16[1024,256]{1,0:T(8,128)(2,1)} copy(bf16[1024,256]{1,0:T(8,128)(2,1)} %get-tuple-element.14) | data formatting | bytes 1048576
  (2 shorter events, 0.0 us)
Async XLA Ops:
  84.2 11.1 %copy-start = (f32[7,1024]{1,0:T(8,128)S(1)}, f32[7,1024]{1,0:T(8,128)}, u32[]{:S(2)}) copy-start(f32[7,1024]{1,0:T(8,128)} %param.19) | copy-start | bytes 86020

commit v4 on v3

--- a/solution.py
+++ b/solution.py
@@ -54,11 +54,14 @@
     reward_ref,
     frames_ref,
     slope_ref,
-    head_ref,
+    pooled_ref,
+    embed_ref,
     weight_ref,
     logprob_ref,
     out_ref,
     grad_head_ref,
+    head_rows,
+    head_ref,
     logits_send,
     logits_all,
     stats_send,
@@ -111,6 +114,12 @@
             stats = stats + jnp.where(lane == 3 * group_count, valid, 0.0)
     stats_send[...] = stats
     stats_all[group] = stats
+    head_rows[...] = jnp.zeros_like(head_rows)
+    for episode in range(episodes):
+        head_rows[episode * action_count : (episode + 1) * action_count, :] = (
+            pooled_ref[episode : episode + 1, :] + embed_ref[...]
+        )
+    head_ref[...] = head_rows[...].astype(jnp.bfloat16)
     partial = jnp.dot(head_ref[...], weight_ref[...], preferred_element_type=jnp.float32)
     logits_send[...] = partial
     logits_all[me] = partial
@@ -333,13 +342,13 @@
         to_all(grad_send, grad_all, grad_sems, step, group, (me, peer)).wait_send()
 
 
-def tail(actions, action_mask, group_ids, rewards, frames, slopes, head_input, head_weight):
+def tail(actions, action_mask, group_ids, rewards, frames, slopes, pooled, act_embed, head_weight):
     n_cp, n_grp = lax.axis_size("cp"), lax.axis_size("grp")
     n_out = n_grp // 2
     episodes = actions.shape[0]
     group_count = max(1, episodes * n_grp // 8)
     features, width = frames.shape[2], slopes.shape[2]
-    rows, bins = head_input.shape[0], head_weight.shape[1]
+    rows, bins = -(-actions.size // 16) * 16, head_weight.shape[1]
     chunk, parts = features // n_grp, 2
     in_smem = pl.BlockSpec(memory_space=pltpu.SMEM)
     in_vmem = pl.BlockSpec(memory_space=pltpu.VMEM)
@@ -352,9 +361,11 @@
             jax.ShapeDtypeStruct((chunk, width), jnp.bfloat16),
             jax.ShapeDtypeStruct((width, bins), jnp.bfloat16),
         ),
-        in_specs=[in_smem] * 4 + [in_vmem] * 4,
+        in_specs=[in_smem] * 4 + [in_vmem] * 5,
         out_specs=(in_vmem,) * 3,
         scratch_shapes=[
+            pltpu.VMEM((rows, width), jnp.float32),
+            pltpu.VMEM((rows, width), jnp.bfloat16),
             pltpu.VMEM((rows, bins), jnp.float32),
             pltpu.VMEM((n_cp, rows, bins), jnp.float32),
             pltpu.VMEM((8, 128), jnp.float32),
@@ -373,7 +384,7 @@
             collective_id=1, has_side_effects=True, vmem_limit_bytes=60 * 1024 * 1024
         ),
         name="tail",
-    )(actions, action_mask, group_ids, rewards, frames, slopes, head_input, head_weight)
+    )(actions, action_mask, group_ids, rewards, frames, slopes, pooled, act_embed, head_weight)
 
 
 def front_kernel(
@@ -387,6 +398,7 @@
     shard_ref,
     frames_ref,
     columns_ref,
+    scale_ref,
     heads_all,
     blocks,
     map_held,
@@ -471,6 +483,11 @@
             (peer, group),
         )
 
+    for episode in range(episodes):
+        length = jnp.full((1, seq), length_ref[episode], jnp.int32)
+        kept = lax.broadcasted_iota(jnp.int32, (1, seq), 1) < length
+        scale_ref[episode : episode + 1, :] = jnp.where(kept, 1.0 / length.astype(jnp.float32), 0.0)
+
     strip = min(seq, 256)
 
     def attend(episode):
@@ -549,9 +566,10 @@
             block_copy(episode, 2, row_peer, col_peer, 0, half, 0).start()
             block_copy(episode, 1, col_peer, col_peer, 0, seq, 0).wait_recv()
             block_copy(episode, 3, col_peer, row_peer, half, half, 1).start()
+            if episode == 0:
+                forward_shards()
             add_frames(episode, row_peer, False, False)
             add_frames(episode, col_peer, False, False)
-        forward_shards()
         for episode in range(episodes):
             block_copy(episode, 2, far_peer, col_peer, 0, half, 0).wait_recv()
             block_copy(episode, 3, far_peer, row_peer, half, half, 1).wait_recv()
@@ -595,14 +613,15 @@
     anywhere = pl.BlockSpec(memory_space=pl.ANY)
     in_vmem = pl.BlockSpec(memory_space=pltpu.VMEM)
     dma = pltpu.SemaphoreType.DMA
-    frames, columns = pl.pallas_call(
+    frames, columns, token_scale = pl.pallas_call(
         lambda *refs: front_kernel(n_cp, n_out, *refs),
         out_shape=(
             jax.ShapeDtypeStruct((episodes, seq, features), jnp.bfloat16),
             jax.ShapeDtypeStruct((n_grp, chunk, cols), jnp.bfloat16),
+            jax.ShapeDtypeStruct((episodes, seq), jnp.float32),
         ),
         in_specs=[pl.BlockSpec(memory_space=pltpu.SMEM)] + [anywhere] * 4 + [in_vmem],
-        out_specs=(in_vmem, anywhere),
+        out_specs=(in_vmem, anywhere, in_vmem),
         scratch_shapes=[
             pltpu.VMEM((3, episodes, seq, width), jnp.bfloat16),
             pltpu.VMEM((n_cp, episodes * seq, width), jnp.bfloat16),
@@ -623,7 +642,24 @@
         ),
         name="front",
     )(lengths, queries, keys, values, frame_map, proj_weight)
-    return frames, columns.reshape(n_grp * chunk, cols)
+    return frames, columns.reshape(n_grp * chunk, cols), token_scale
+
+
+def write_kernel(first, second, third, first_out, second_out, third_out):
+    first_out[...] = first[...]
+    second_out[...] = second[...]
+    third_out[...] = third[...]
+
+
+def write_out(*results):
+    in_vmem = pl.BlockSpec(memory_space=pltpu.VMEM)
+    return pl.pallas_call(
+        write_kernel,
+        out_shape=tuple(jax.ShapeDtypeStruct(result.shape, result.dtype) for result in results),
+        in_specs=[in_vmem] * 3,
+        out_specs=(in_vmem,) * 3,
+        name="write_out",
+    )(*results)
 
 
 def per_device(
@@ -641,9 +677,7 @@
     rewards,
 ):
     episodes_here, tokens_here, att_width = queries.shape
-    action_count = act_embed.shape[0]
-    lengths_real = lengths.astype(jnp.float32)
-    all_frames, proj_cols = front(queries, keys, values, lengths, frame_map, proj_weight)
+    all_frames, proj_cols, token_scale = front(queries, keys, values, lengths, frame_map, proj_weight)
     seq_span = all_frames.shape[1]
     flat_frames = all_frames.reshape(episodes_here * seq_span, all_frames.shape[2])
     col_count = proj_cols.shape[1]
@@ -651,15 +685,8 @@
         episodes_here, seq_span, col_count
     )
     hidden = gelu_exact(pre_act)
-    token_mask = (jnp.arange(seq_span, dtype=jnp.int32)[None, :] < lengths[:, None]).astype(
-        jnp.float32
-    )
-    pooled = jnp.sum(token_mask[:, :, None] * hidden, axis=1) / lengths_real[:, None]
-    sum_input = pooled[:, None, :] + act_embed[None, :, :]
-    head_input = sum_input.astype(jnp.bfloat16).reshape(episodes_here * action_count, col_count)
-    spare = -head_input.shape[0] % 16
-    scaled_mask = token_mask / lengths_real[:, None]
-    slopes = (scaled_mask[:, :, None] * gelu_slope(pre_act)).astype(jnp.bfloat16)
+    pooled = jnp.sum(token_scale[:, :, None] * hidden, axis=1)
+    slopes = (token_scale[:, :, None] * gelu_slope(pre_act)).astype(jnp.bfloat16)
     logprobs, grad_proj, grad_head = tail(
         actions,
         action_mask,
@@ -667,10 +694,11 @@
         rewards,
         all_frames,
         slopes,
-        jnp.pad(head_input, ((0, spare), (0, 0))),
+        pooled,
+        act_embed,
         head_weight,
     )
-    return (logprobs, grad_proj, grad_head)
+    return write_out(logprobs, grad_proj, grad_head)
 
 
 def solution(mesh):

time: 155 us -> 150 us (0.968)
  local copies, waits for them, and re-layouts: 5.64 us -> 0 us
  other arithmetic: 2.2 us -> 0 us
  Pallas kernels: 136 us -> 138 us
    unnamed x5 -> x0, local copies, waits for them, and re-layouts: 5 us -> none
    pallas_call x0 -> x1, Pallas kernels: none -> 2.23 us  [write_out(): pl.pallas_call(write_kernel, out_shape=tuple((jax.ShapeDtypeStruct(result...]
where the time goes in v4:
time: 150 us
  Pallas kernels  138 us (92%)
  matrix products  11.5 us (8%)
    pallas_call x1, Pallas kernels, front(): pl.pallas_call(lambda *refs: front_kernel(n_cp, n_out, *refs), out_shape=...  81.5 us
    pallas_call x1, Pallas kernels, tail(): pl.pallas_call(lambda *refs: tail_kernel(n_cp, n_out, group_count, *refs)...  54.2 us
    dot_general x1, matrix products, per_device(): jnp.dot(flat_frames, proj_cols, preferred_element_type=jnp.float32)  11.5 us

profile of v4, /device:TPU:0, one launch (start us, length us, event | category | flops | bytes accessed | tf_op | source)
XLA Modules:
  0.0 150.1 jit_solution(2203574584033279181)
XLA Ops:
  0.6 81.5 %front.1 = (bf16[2,512,2176]{2,1,0:T(8,128)(2,1)}, bf16[8,272,1024]{2,1,0:T(8,128)(2,1)}, f32[2,512]{1,0:T(2,128)}) custom-call(s32[2]{0:T(128)} %refs_0_.2, bf16[2,128,2048]{2,1,0:T(8,128)(2,1)} %refs_1_.2, bf16[2,128,2048]{2,1,0:T(8,128)(2,1)} %refs_2_.2, bf16[2,128,2048]{2,1,0:T(8,128)(2,1)} %refs_3_.2, bf16[2048,2176]{1,0:T(8,128)(2,1)} %refs_4_.1, ...), custom_call_target="tpu_custom_call" | custom-call | tf_op jit(solution)/shard_map/front/pallas_call | solution.py:616
  82.2 11.5 %multiply_reduce_fusion = (f32[2,1024]{1,0:T(2,128)}, bf16[2,512,1024]{2,1,0:T(8,128)(2,1)}) fusion(f32[2,512]{1,0:T(2,128)} %get-tuple-element.10, bf16[2,512,2176]{2,1,0:T(8,128)(2,1)} %get-tuple-element.9.refs_4_, bf16[2176,1024,1]{1,0,2:T(8,128)(2,1)} %bitcast.5), kind=kOutput, calls=%fused_computation.7 | convolution fusion | flops 4578080768 | bytes 11022336 | tf_op jit(solution)/shard_map/dot_general | solution.py:684
  93.7 54.2 %tail.1 = (f32[2,7]{1,0:T(2,128)}, bf16[272,1024]{1,0:T(8,128)(2,1)}, bf16[1024,256]{1,0:T(8,128)(2,1)}) custom-call(s32[2,7]{1,0:T(2,128)} %refs_0_.3, s32[2,7]{1,0:T(2,128)} %refs_1_.3, s32[2]{0:T(128)} %refs_2_.3, f32[2]{0:T(128)} %refs_3_.3, bf16[2,512,2176]{2,1,0:T(8,128)(2,1)} %get-tuple-element.9.refs_4_, ...), custom_call_target="tpu_custom_call" | custom-call | tf_op jit(solution)/shard_map/tail/pallas_call | solution.py:357
  147.9 2.2 %write_out.1 = (f32[2,7]{1,0:T(2,128)}, bf16[272,1024]{1,0:T(8,128)(2,1)}, bf16[1024,256]{1,0:T(8,128)(2,1)}) custom-call(f32[2,7]{1,0:T(2,128)} %get-tuple-element.12.first, bf16[272,1024]{1,0:T(8,128)(2,1)} %get-tuple-element.13.second, bf16[1024,256]{1,0:T(8,128)(2,1)} %get-tuple-element.14.third), custom_call_target="tpu_custom_call" | custom-call | tf_op jit(solution)/shard_map/write_out/pallas_call | solution.py:656

commit v5 on v4

--- a/solution.py
+++ b/solution.py
@@ -349,7 +349,7 @@
     group_count = max(1, episodes * n_grp // 8)
     features, width = frames.shape[2], slopes.shape[2]
     rows, bins = -(-actions.size // 16) * 16, head_weight.shape[1]
-    chunk, parts = features // n_grp, 2
+    chunk, parts = features // n_grp, 4
     in_smem = pl.BlockSpec(memory_space=pltpu.SMEM)
     in_vmem = pl.BlockSpec(memory_space=pltpu.VMEM)
     dma = pltpu.SemaphoreType.DMA

time: 150 us -> 152 us (1.013)
  no operation moved by 1% of the time
where the time goes in v5:
time: 152 us
  Pallas kernels  139 us (91%)
  matrix products  11.5 us (8%)
    pallas_call x1, Pallas kernels, front(): pl.pallas_call(lambda *refs: front_kernel(n_cp, n_out, *refs), out_shape=...  81.5 us
    pallas_call x1, Pallas kernels, tail(): pl.pallas_call(lambda *refs: tail_kernel(n_cp, n_out, group_count, *refs)...  55.6 us
    dot_general x1, matrix products, per_device(): jnp.dot(flat_frames, proj_cols, preferred_element_type=jnp.float32)  11.5 us

profile of v5, /device:TPU:0, one launch (start us, length us, event | category | flops | bytes accessed | tf_op | source)
XLA Modules:
  0.0 151.6 jit_solution(17119279097948048313)
XLA Ops:
  0.6 81.5 %front.1 = (bf16[2,512,2176]{2,1,0:T(8,128)(2,1)}, bf16[8,272,1024]{2,1,0:T(8,128)(2,1)}, f32[2,512]{1,0:T(2,128)}) custom-call(s32[2]{0:T(128)} %refs_0_.2, bf16[2,128,2048]{2,1,0:T(8,128)(2,1)} %refs_1_.2, bf16[2,128,2048]{2,1,0:T(8,128)(2,1)} %refs_2_.2, bf16[2,128,2048]{2,1,0:T(8,128)(2,1)} %refs_3_.2, bf16[2048,2176]{1,0:T(8,128)(2,1)} %refs_4_.1, ...), custom_call_target="tpu_custom_call" | custom-call | tf_op jit(solution)/shard_map/front/pallas_call | solution.py:616
  82.2 11.5 %multiply_reduce_fusion = (f32[2,1024]{1,0:T(2,128)}, bf16[2,512,1024]{2,1,0:T(8,128)(2,1)}) fusion(f32[2,512]{1,0:T(2,128)} %get-tuple-element.10, bf16[2,512,2176]{2,1,0:T(8,128)(2,1)} %get-tuple-element.9.refs_4_, bf16[2176,1024,1]{1,0,2:T(8,128)(2,1)} %bitcast.5), kind=kOutput, calls=%fused_computation.7 | convolution fusion | flops 4578080768 | bytes 11022336 | tf_op jit(solution)/shard_map/dot_general | solution.py:684
  93.7 55.6 %tail.1 = (f32[2,7]{1,0:T(2,128)}, bf16[272,1024]{1,0:T(8,128)(2,1)}, bf16[1024,256]{1,0:T(8,128)(2,1)}) custom-call(s32[2,7]{1,0:T(2,128)} %refs_0_.3, s32[2,7]{1,0:T(2,128)} %refs_1_.3, s32[2]{0:T(128)} %refs_2_.3, f32[2]{0:T(128)} %refs_3_.3, bf16[2,512,2176]{2,1,0:T(8,128)(2,1)} %get-tuple-element.9.refs_4_, ...), custom_call_target="tpu_custom_call" | custom-call | tf_op jit(solution)/shard_map/tail/pallas_call | solution.py:357
  149.3 2.2 %write_out.1 = (f32[2,7]{1,0:T(2,128)}, bf16[272,1024]{1,0:T(8,128)(2,1)}, bf16[1024,256]{1,0:T(8,128)(2,1)}) custom-call(f32[2,7]{1,0:T(2,128)} %get-tuple-element.12.first, bf16[272,1024]{1,0:T(8,128)(2,1)} %get-tuple-element.13.second, bf16[1024,256]{1,0:T(8,128)(2,1)} %get-tuple-element.14.third), custom_call_target="tpu_custom_call" | custom-call | tf_op jit(solution)/shard_map/write_out/pallas_call | solution.py:656
